TPU v7x, 512 devices: a whole 4x4x16 slice. The times are simulated.
512 devices in a mesh: row: 64 (over z, y), col: 8 (over x, core).
Axes of the slice: x: 4, y: 4, z: 16, core: 2. Of those that a mesh axis runs over, the one named last changes fastest.
Arguments:
- traces: float32 [16, 32768], P('col', 'row'), may hold values from -50 to 50
Outputs:
- overwritten: float32 [32768, 4096], P('row', 'col')
- coupling: float32 [256, 4096], P(None, 'col')
All inputs are finite; a program needn't handle non-finite values.
Results may differ from a plain program's by a relative error of at most 0.0015.
Values sent between devices are 32-bit elements; how exact they have to be, the bound alone decides.
A program may use at most 64 MiB of HBM per device.

v0:
```python
import jax
import jax.numpy as jnp
from jax import lax
from jax.sharding import PartitionSpec as P

TAPS = 256
PANEL = 128
NPAN = 2
WIDE = 256


def from_behind(value, axis, steps):
    count = lax.axis_size(axis)
    leading, last = (max(0, -steps), min(count, count - steps))
    return lax.ppermute(value, axis, [(source, source + steps) for source in range(leading, last)])


def from_root(value, axis, source):
    kept = jnp.where(lax.axis_index(axis) == source, value, 0).astype(value.dtype)
    return lax.psum(kept, axis)


def hankel_piece(segment, row_count, col_count):
    length = segment.shape[-1]
    flipped = jnp.flip(segment, -1)
    repeated = jnp.tile(flipped, (1, row_count + 1))[:, : row_count * (length + 1)]
    hankel_table = repeated.reshape(segment.shape[0], row_count, length + 1)[:, :, :col_count]
    return jnp.flip(hankel_table, 1)


def toeplitz_local(extended, tap_count, col_count):
    rows_total = extended.shape[1] - tap_count
    step_rows = min(512, rows_total)
    pieces = hankel_piece(extended, step_rows, col_count)
    return pieces


def triangle_inverse(gram_part):
    factor_low = jnp.linalg.cholesky(gram_part)
    return jax.scipy.linalg.solve_triangular(
        factor_low, jnp.eye(gram_part.shape[0], dtype=jnp.float32), lower=True
    )


def body(traces):
    highest = lax.Precision.HIGHEST
    rows_here = traces.shape[1]
    total_rows = rows_here * lax.axis_size("row")
    history = from_behind(traces[:, rows_here - TAPS :], "row", 1)
    extended = jnp.concatenate([history, traces], axis=1)
    local_taps = toeplitz_local(extended, TAPS, TAPS)
    matrix = jnp.transpose(local_taps, (1, 0, 2)).reshape(rows_here, -1)
    group_cols = matrix.shape[1]
    source = from_root(extended[0:1], "col", 0)
    panel_cols = toeplitz_local(source, TAPS, WIDE)[0]
    remainder = matrix
    trailing = panel_cols
    basis_list = []
    coupling_list = []
    for number in range(NPAN):
        current = trailing[:, :PANEL]
        ahead_local = jnp.dot(current.T, trailing, precision=highest)
        cross_local = jnp.dot(current.T, remainder, precision=highest)
        ahead_sum, cross_sum = lax.psum((ahead_local, cross_local), "row")
        inverse = triangle_inverse(ahead_sum[:, :PANEL] / total_rows)
        basis_part = jnp.dot(current, inverse.T, precision=highest)
        ahead_coupled = jnp.dot(inverse, ahead_sum[:, PANEL:] / total_rows, precision=highest)
        cross_coupled = jnp.dot(inverse, cross_sum / total_rows, precision=highest)
        trailing = trailing[:, PANEL:] - jnp.dot(basis_part, ahead_coupled, precision=highest)
        remainder = remainder - jnp.dot(basis_part, cross_coupled, precision=highest)
        basis_list.append(basis_part)
        coupling_list.append(cross_coupled)
    basis_cols = jnp.concatenate(basis_list, axis=1)
    coupling = jnp.concatenate(coupling_list, axis=0)
    columns = lax.axis_index("col") * group_cols + jnp.arange(group_cols)
    placed = jnp.concatenate(
        [basis_cols, jnp.zeros((rows_here, group_cols - WIDE), jnp.float32)], axis=1
    )
    overwritten = jnp.where((columns < WIDE)[None, :], placed, remainder)
    return (overwritten, coupling)


def solution(mesh):
    return jax.shard_map(
        body,
        mesh=mesh,
        in_specs=(P("col", "row"),),
        out_specs=(P("row", "col"), P(None, "col")),
        check_vma=False,
    )
```

profile of v0, /device:TPU:2, one launch (start us, length us, event | category | flops | bytes accessed | tf_op | source)
XLA Modules:
  0.0 657.5 jit_solution(10858557208293177267)
XLA Ops:
  7.2 0.7 slice.38
  7.9 3.5 collective-permute-start
  11.4 1.3 collective-permute-done
  12.7 0.7 constant_dynamic-update-slice_fusion
  14.1 1.6 copy.20
  16.0 6.8 %reshape.37 = f32[2,512,769]{2,1,0:T(8,128)} reshape(f32[2,393728]{1,0:T(2,128)S(1)} %slice.55) | data formatting | bytes 6299648 | tf_op jit(solution)/shard_map/reshape | solution.py:27
  22.8 1.2 slice-done
  25.3 12.8 %psum.35 = f32[768]{0:T(1024)S(1)} all-reduce(f32[768]{0:T(1024)S(1)} %reduce.4), channel_id=1, replica_groups=mesh['row'=64,'col'=8] {'col'}, use_global_device_ids=true, to_apply=%region_0.1 | all-reduce | flops 768 | bytes 6144 | tf_op jit(solution)/shard_map/psum | solution.py:20
  38.2 1.6 copy.19
  39.9 16.2 %slice_reduce_fusion = f32[393728]{0:T(1024)S(1)} fusion(f32[1,393984]{1,0:T(1,128)S(1)} %bitcast.54), kind=kLoop, calls=%fused_computation.1 | loop fusion | bytes 3149824 | tf_op jit(solution)/shard_map/slice | solution.py:26
  56.1 2.8 reshape.36
  58.9 1.1 slice.50
  60.3 1.7 fusion.9
  61.9 1.5 fusion.5
  63.7 268.6 %all-reduce.7.cloned.1.call-done = (f32[128,256]{0,1:T(8,128)}, f32[128,512]{1,0:T(8,128)}) async-done(((f32[128,256]{0,1:T(8,128)}, f32[128,512]{1,0:T(8,128)}), (f32[128,256]{0,1:T(8,128)}, f32[128,512]{1,0:T(8,128)})) %all-reduce.7.cloned.1.call-update) | async-done | bytes 393232 | tf_op jit(solution)/shard_map/psum | solution.py:64
  332.3 0.9 slice_multiply_fusion.2
  333.3 0.9 fusion.23
  334.1 11.7 %cholesky.44 = f32[128,128]{1,0:T(8,128)S(1)} custom-call(f32[128,128]{1,0:T(8,128)S(1)} %fusion.23), custom_call_target="Cholesky" | custom-call | tf_op jit(solution)/shard_map/jit(cholesky)/cholesky | solution.py:39
  347.2 9.8 %custom-call.6 = f32[1,128,128]{1,2,0:T(8,128)S(1)} custom-call(f32[1,128,128]{2,1,0:T(8,128)S(1)} %fusion.17), custom_call_target="InvertDiagBlocksLowerTriangular" | custom-call | tf_op jit(solution)/shard_map/jit(_solve_triangular)/triangular_solve | solution.py:40
  357.7 1.1 fusion.19
  359.2 1.0 convolution_subtract_fusion.1
  360.8 1.2 fusion.28
  362.1 1.5 fusion.30
  363.7 257.0 %all-reduce.5.cloned.1.call-done = (f32[128,128]{0,1:T(8,128)}, f32[128,512]{1,0:T(8,128)}) async-done(((f32[128,128]{0,1:T(8,128)}, f32[128,512]{1,0:T(8,128)}), (f32[128,128]{0,1:T(8,128)}, f32[128,512]{1,0:T(8,128)})) %all-reduce.5.cloned.1.call-update) | async-done | bytes 327696 | tf_op jit(solution)/shard_map/psum | solution.py:64
  620.8 0.8 broadcast_multiply_fusion
  621.7 0.9 fusion.21
  622.6 11.9 %cholesky.55 = f32[128,128]{1,0:T(8,128)S(1)} custom-call(f32[128,128]{1,0:T(8,128)S(1)} %fusion.21), custom_call_target="Cholesky" | custom-call | tf_op jit(solution)/shard_map/jit(cholesky)/cholesky | solution.py:39
  635.2 0.7 fusion.18
  635.8 9.8 %custom-call.7 = f32[1,128,128]{1,2,0:T(8,128)S(1)} custom-call(f32[1,128,128]{2,1,0:T(8,128)S(1)} %fusion.18), custom_call_target="InvertDiagBlocksLowerTriangular" | custom-call | tf_op jit(solution)/shard_map/jit(_solve_triangular)/triangular_solve | solution.py:40
  646.3 1.3 fusion.1
  647.8 0.8 pad_maximum_fusion
  648.6 2.0 fusion
  (36 shorter events, 7.7 us)
Async XLA Ops:
  7.2 325.1 %all-reduce.7.cloned.1.call-start = ((), (), s32[]{:S(2)}) async-start(), calls=%async_computation.1 | async-start | bytes 786432 | tf_op jit(solution)/shard_map/psum | solution.py:64
  7.9 4.8 collective-permute-start
  22.8 1.2 slice-start
  63.4 557.3 %all-reduce.5.cloned.1.call-start = ((), (), s32[]{:S(2)}) async-start(), calls=%async_computation | async-start | bytes 655360 | tf_op jit(solution)/shard_map/psum | solution.py:64
  332.3 26.5 %copy-start = (f32[128,512]{1,0:T(8,128)S(1)}, f32[128,512]{1,0:T(8,128)}, u32[]{:S(2)}) copy-start(f32[128,512]{1,0:T(8,128)} %get-tuple-element.7) | copy-start | bytes 786436
Sparse Core Ops, SparseCore 0:
  63.5 268.7 all-reduce.6
  363.7 257.0 all-reduce.4
where the time goes:
time: 658 us; the launch traced here: 657 us
  waiting for transfers between devices  527 us (80%)
  other arithmetic  50.2 us (8%)
  local copies, waits for them, and re-layouts  35.8 us (5%)
  between operations  14.3 us (2%)
  matrix products  13.6 us (2%)
  blocking collectives  12.8 us (2%)
    psum x2, waiting for transfers between devices, body(): ahead_sum, cross_sum = lax.psum((ahead_local, cross_local), 'row')  526 us
    another operation x6, other arithmetic, triangle_inverse(): factor_low = jnp.linalg.cholesky(gram_part)  25 us
    another operation x4, other arithmetic, triangle_inverse(): jax.scipy.linalg.solve_triangular(factor_low, jnp.eye(gram_part.shape[0],...  20.9 us
    slice x2, local copies, waits for them, and re-layouts, hankel_piece(): jnp.tile(flipped, (1, row_count + 1))[:, :row_count * (length + 1)]  16.5 us
  transfers between devices with their start and end apart: 3, of which 3 were waited for; matrix products, arithmetic and copies ran while one was open for 0% of the time, Pallas kernels for 0%

commit v1 on v0

v1 whole, which is shorter than its diff:
```python
import functools

import jax
import jax.numpy as jnp
from jax import lax
from jax.experimental import pallas as pl
from jax.experimental.pallas import tpu as pltpu
from jax.sharding import PartitionSpec as P

TAPS = 256
WIDE = 256
SLAB = 4
MESH = pl.DeviceIdType.MESH
HIGHEST = lax.Precision.HIGHEST
VM = pl.BlockSpec(memory_space=pltpu.VMEM)


def dot(a, b, da=1, db=0):
    return lax.dot_general(
        a, b, (((da,), (db,)), ((), ())), precision=HIGHEST, preferred_element_type=jnp.float32
    )


def iota(shape, axis):
    return lax.broadcasted_iota(jnp.int32, shape, axis)


def anti_identity():
    return jnp.where(iota((128, 128), 0) + iota((128, 128), 1) == 127, 1.0, 0.0).astype(jnp.float32)


def lag_kernel(
    slabs, cols,
    x_ref, sums_ref, ext_ref, tail_ref,
    own0, slab0, slabc, before0, after0, beforec, tail0, tailc, lags,
    local_sem, send_x, recv_x, send_0, recv_0, send_hc, recv_hc,
    send_s0, recv_s0, send_hb, recv_hb, send_ha, recv_ha, send_t, recv_t, send_l, recv_l,
):
    row, col = lax.axis_index("row"), lax.axis_index("col")
    z, y = row // SLAB, row % SLAB
    rows = x_ref.shape[1]
    cut = rows - TAPS
    first, last = y == 0, y == SLAB - 1
    has_before, has_after = z > 0, z < slabs - 1
    in_tail = z == slabs - 1

    def at(zz, yy, cc):
        return (zz * SLAB + yy, cc)

    def remote(src, dst, send, recv, where):
        return pltpu.make_async_remote_copy(
            src_ref=src, dst_ref=dst, send_sem=send, recv_sem=recv, device_id=where, device_id_type=MESH
        )

    barrier = pltpu.get_barrier_semaphore()

    def greet(where):
        pl.semaphore_signal(barrier, inc=1, device_id=where, device_id_type=MESH)

    @pl.loop(1, slabs)
    def _(k):
        greet(at((z + k) % slabs, y, col))

    for k in range(1, SLAB):
        greet(at(z, (y + k) % SLAB, col))

    @pl.when(col == 0)
    def _():
        for k in range(1, cols):
            greet(at(z, y, k))

    @pl.when(col != 0)
    def _():
        greet(at(z, y, 0))

    @pl.when(last & has_after)
    def _():
        for k in range(SLAB):
            greet(at(z + 1, k, col))

    @pl.when(first & has_before)
    def _():
        for k in range(SLAB):
            greet(at(z - 1, k, col))

    @pl.when(has_before)
    def _():
        greet(at(z - 1, SLAB - 1, col))

    @pl.when(has_after)
    def _():
        greet(at(z + 1, 0, col))

    def yes(flag):
        return jnp.where(flag, 1, 0)

    expected = (
        slabs - 1 + SLAB - 1 + 1 + (cols - 2) * yes(col == 0)
        + SLAB * yes(last & has_after) + SLAB * yes(first & has_before)
        + yes(has_before) + yes(has_after)
    )

    @pl.when(z == 0)
    def _():
        before0[...] = jnp.zeros_like(before0)
        beforec[...] = jnp.zeros_like(beforec)

    @pl.when(in_tail)
    def _():
        after0[...] = jnp.zeros_like(after0)

    keep_c = pltpu.make_async_copy(x_ref, slabc.at[y], local_sem.at[0])
    keep_c.start()
    pl.semaphore_wait(barrier, expected)

    @pl.when(col == 0)
    def _():
        for k in range(1, cols):
            remote(x_ref.at[0:1, :], own0.at[0:1, :], send_0.at[k], recv_0.at[0], at(z, y, k)).start()
        own = pltpu.make_async_copy(x_ref.at[0:1, :], own0.at[0:1, :], local_sem.at[1])
        own.start()
        own.wait()

    for k in range(1, SLAB):
        remote(x_ref, slabc.at[y], send_x.at[k], recv_x.at[y], at(z, (y + k) % SLAB, col)).start()

    @pl.when(last & has_after)
    def _():
        remote(x_ref.at[:, cut:], beforec, send_hc.at[0], recv_hc.at[0], at(z + 1, 0, col)).start()

    @pl.when(col != 0)
    def _():
        remote(x_ref.at[0:1, :], own0.at[0:1, :], send_0.at[0], recv_0.at[0], at(z, y, 0)).wait_recv()

    keep_0 = pltpu.make_async_copy(own0.at[0:1, :], slab0.at[y, 0:1, :], local_sem.at[2])
    keep_0.start()
    for k in range(1, SLAB):
        remote(
            own0.at[0:1, :], slab0.at[y, 0:1, :], send_s0.at[k], recv_s0.at[y], at(z, (y + k) % SLAB, col)
        ).start()

    @pl.when(last & has_after)
    def _():
        for k in range(SLAB):
            remote(
                own0.at[0:1, cut:], before0.at[0:1, :], send_hb.at[k], recv_hb.at[0], at(z + 1, k, col)
            ).start()

    @pl.when(first & has_before)
    def _():
        for k in range(SLAB):
            remote(
                own0.at[0:1, :TAPS], after0.at[0:1, :], send_ha.at[k], recv_ha.at[0], at(z - 1, k, col)
            ).start()

    keep_c.wait()
    keep_0.wait()
    for k in range(1, SLAB):
        other = (y + k) % SLAB
        remote(x_ref, slabc.at[other], send_x.at[k], recv_x.at[other], at(z, other, col)).wait_recv()
        remote(
            own0.at[0:1, :], slab0.at[other, 0:1, :], send_s0.at[k], recv_s0.at[other], at(z, other, col)
        ).wait_recv()

    @pl.when(has_before)
    def _():
        remote(own0.at[0:1, cut:], before0.at[0:1, :], send_hb.at[0], recv_hb.at[0], at(z, y, col)).wait_recv()

    @pl.when(has_after)
    def _():
        remote(own0.at[0:1, :TAPS], after0.at[0:1, :], send_ha.at[0], recv_ha.at[0], at(z, y, col)).wait_recv()

    def tails(k):
        where = at((z + k) % slabs, y, col)
        return (
            remote(slab0.at[SLAB - 1, 0:1, cut:], tail0.at[0:1, :], send_t.at[0, k], recv_t.at[0], where),
            remote(slabc.at[SLAB - 1, :, cut:], tailc, send_t.at[1, k], recv_t.at[1], where),
        )

    @pl.when(in_tail)
    def _():
        @pl.loop(1, slabs)
        def _(k):
            for copy in tails(k):
                copy.start()

        tail0[0:1, :] = slab0[SLAB - 1, 0:1, cut:]
        tailc[...] = slabc[SLAB - 1, :, cut:]

    per = rows // 128
    count = SLAB * per
    block0 = [before0[0:1, 0:128], before0[0:1, 128:256]]
    for j in range(SLAB):
        block0 += [slab0[j, 0:1, 128 * b : 128 * b + 128] for b in range(per)]
    block0 += [after0[0:1, 0:128], after0[0:1, 128:256]]
    ext0 = jnp.concatenate(block0, axis=0)
    wide0 = jnp.concatenate([ext0[k : k + count] for k in range(5)], axis=1)
    place = iota((count, 640), 0) * 128 + iota((count, 640), 1) - 256
    late = count * 128 - (TAPS - 1)
    wide0_early = jnp.where(in_tail & (place >= late), 0.0, wide0)
    right = jnp.concatenate([wide0, wide0_early[count - 8 :]], axis=0)
    flip = anti_identity()
    at_late = in_tail & (iota((count, 128), 0) * 128 + iota((count, 128), 1) >= late)
    lefts = []
    for t in range(3):
        if t == 0:
            mine = ext0[2 : 2 + count]
        else:
            mine = jnp.concatenate(
                [slabc[j, t - 1 : t, 128 * b : 128 * b + 128] for j in range(SLAB) for b in range(per)], axis=0
            )
        lefts += [jnp.where(at_late, 0.0, mine), jnp.where(at_late, mine, 0.0)[count - 8 :]]
    flipped = dot(jnp.concatenate(lefts, axis=0), flip)
    deep = count + 8
    for t in range(3):
        table = dot(flipped[deep * t : deep * t + deep], right, 0, 0)
        skewed = pltpu.roll(table, 1, 1, stride=1, stride_axis=0)
        summed = jnp.sum(skewed, axis=0, keepdims=True)
        for b in range(4):
            lags[z, 4 * t + b : 4 * t + b + 1, :] = summed[:, 128 + 128 * b : 256 + 128 * b]

    def exchange(k):
        where = at((z + k) % slabs, y, col)
        return remote(lags.at[z], lags.at[z], send_l.at[k], recv_l.at[z], where)

    @pl.loop(1, slabs)
    def _(k):
        exchange(k).start()

    ext_ref[0:1, TAPS:] = own0[0:1, :]
    ext_ref[1:3, TAPS:] = x_ref[...]

    @pl.when(first)
    def _():
        ext_ref[0:1, :TAPS] = before0[0:1, :]

        @pl.when(has_before)
        def _():
            remote(x_ref.at[:, cut:], beforec, send_hc.at[0], recv_hc.at[0], at(z, y, col)).wait_recv()

        ext_ref[1:3, :TAPS] = beforec[...]

    @pl.when(y > 0)
    def _():
        ext_ref[0:1, :TAPS] = slab0[(y + SLAB - 1) % SLAB, 0:1, cut:]
        ext_ref[1:3, :TAPS] = slabc[(y + SLAB - 1) % SLAB, :, cut:]

    @pl.when(z < slabs - 1)
    def _():
        for copy in tails(0):
            copy.wait_recv()

    tail_ref[0:1, :] = tail0[0:1, :]
    tail_ref[1:3, :] = tailc[...]

    @pl.loop(1, slabs)
    def _(k):
        other = (z + k) % slabs
        remote(lags.at[other], lags.at[other], send_l.at[k], recv_l.at[other], at(other, y, col)).wait_recv()

    total = lags[0]
    for k in range(1, slabs):
        total = total + lags[k]
    sums_ref[...] = total

    @pl.when(col == 0)
    def _():
        for k in range(1, cols):
            remote(x_ref.at[0:1, :], own0.at[0:1, :], send_0.at[k], recv_0.at[0], at(z, y, k)).wait_send()

    for k in range(1, SLAB):
        other = (y + k) % SLAB
        remote(x_ref, slabc.at[y], send_x.at[k], recv_x.at[y], at(z, other, col)).wait_send()
        remote(
            own0.at[0:1, :], slab0.at[y, 0:1, :], send_s0.at[k], recv_s0.at[y], at(z, other, col)
        ).wait_send()

    @pl.when(last & has_after)
    def _():
        remote(x_ref.at[:, cut:], beforec, send_hc.at[0], recv_hc.at[0], at(z + 1, 0, col)).wait_send()
        for k in range(SLAB):
            remote(
                own0.at[0:1, cut:], before0.at[0:1, :], send_hb.at[k], recv_hb.at[0], at(z + 1, k, col)
            ).wait_send()

    @pl.when(first & has_before)
    def _():
        for k in range(SLAB):
            remote(
                own0.at[0:1, :TAPS], after0.at[0:1, :], send_ha.at[k], recv_ha.at[0], at(z - 1, k, col)
            ).wait_send()

    @pl.when(in_tail)
    def _():
        @pl.loop(1, slabs)
        def _(k):
            for copy in tails(k):
                copy.wait_send()

    @pl.loop(1, slabs)
    def _(k):
        exchange(k).wait_send()


def lag_sums(traces, slabs, cols):
    rows = traces.shape[1]
    f32, dma = jnp.float32, pltpu.SemaphoreType.DMA
    return pl.pallas_call(
        functools.partial(lag_kernel, slabs, cols),
        name="lag_sums",
        out_shape=(
            jax.ShapeDtypeStruct((12, 128), f32),
            jax.ShapeDtypeStruct((3, rows + TAPS), f32),
            jax.ShapeDtypeStruct((3, TAPS), f32),
        ),
        in_specs=[VM],
        out_specs=(VM, VM, VM),
        scratch_shapes=[
            pltpu.VMEM((2, rows), f32),
            pltpu.VMEM((SLAB, 2, rows), f32),
            pltpu.VMEM((SLAB, 2, rows), f32),
            pltpu.VMEM((2, TAPS), f32),
            pltpu.VMEM((2, TAPS), f32),
            pltpu.VMEM((2, TAPS), f32),
            pltpu.VMEM((2, TAPS), f32),
            pltpu.VMEM((2, TAPS), f32),
            pltpu.VMEM((slabs, 12, 128), f32),
            dma((3,)),
            dma((SLAB,)), dma((SLAB,)),
            dma((cols,)), dma((1,)),
            dma((1,)), dma((1,)),
            dma((SLAB,)), dma((SLAB,)),
            dma((SLAB,)), dma((1,)),
            dma((SLAB,)), dma((1,)),
            dma((2, slabs)), dma((2,)),
            dma((slabs,)), dma((slabs,)),
        ],
        compiler_params=pltpu.CompilerParams(collective_id=0, has_side_effects=True),
    )(traces)


def factor_inverse(work, size):
    sub = iota((8, 128), 0)
    lane = iota((8, size), 1)
    for k in range(size // 8):
        here = work[8 * k : 8 * k + 8, :]
        cols = [jnp.broadcast_to(here[:, 8 * k + j : 8 * k + j + 1], (8, 128)) for j in range(8)]
        invs = [jnp.where(sub == j, 1.0, 0.0).astype(jnp.float32) for j in range(8)]
        for j in range(8):
            scale = lax.rsqrt(jnp.broadcast_to(cols[j][j : j + 1], (8, 128)))
            below = jnp.where(sub > j, cols[j] * scale, 0.0)
            for m in range(j + 1, 8):
                cols[m] = cols[m] - below * (jnp.broadcast_to(cols[m][j : j + 1], (8, 128)) * scale)
            for m in range(j + 1):
                piv = jnp.broadcast_to(invs[m][j : j + 1], (8, 128)) * scale
                invs[m] = jnp.where(sub == j, piv, invs[m] - below * piv)
        done = None
        for m in range(8):
            wide = jnp.concatenate([invs[m]] * (2 * size // 128), axis=1) * jnp.broadcast_to(here[m : m + 1, :], (8, 2 * size))
            done = wide if done is None else done + wide
        work[8 * k : 8 * k + 8, :] = done
        if 8 * k + 8 < size:
            left = jnp.where(lane > 8 * k + 7, done[:, :size], 0.0)
            change = dot(left, done, 0, 0)
            work[8 * k + 8 :, :] = work[8 * k + 8 :, :] - change[8 * k + 8 :, :]


def remainder_kernel(count, sums_ref, ext_ref, tail_ref, over_ref, coup_ref, work, low):
    flip = anti_identity()
    blocks = (ext_ref.shape[1]) // 128
    ext = jnp.concatenate(
        [ext_ref[t : t + 1, 128 * b : 128 * b + 128] for t in range(3) for b in range(blocks)], axis=0
    )
    flipped = dot(ext, flip)

    def toeplitz(t):
        row = jnp.concatenate(
            [flipped[blocks * t + b : blocks * t + b + 1] for b in reversed(range(blocks))], axis=1
        )
        turned = pltpu.roll(jnp.broadcast_to(row, (128, 128 * blocks)), 1, 1, stride=1, stride_axis=0)
        return jnp.concatenate(
            [
                jnp.concatenate([turned[:, 512 - 128 * (s - k) :][:, :128] for k in range(2)], axis=1)
                for s in range(blocks - 2)
            ],
            axis=0,
        )

    zero = jnp.zeros((128, 128), jnp.float32)

    def late(t):
        tail = jnp.where(iota((1, TAPS), 1) == 0, 0.0, tail_ref[t : t + 1, :])
        row = jnp.concatenate([jnp.zeros((1, 128), jnp.float32), tail], axis=1)
        turned = pltpu.roll(jnp.broadcast_to(row, (128, 384)), 0, 1, stride=1, stride_axis=0)
        top = jnp.concatenate([turned[:, 128:256], turned[:, 256:384]], axis=1)
        return jnp.concatenate([top, jnp.concatenate([zero, turned[:, 128:256]], axis=1)], axis=0)

    def early(t):
        row = jnp.concatenate([sums_ref[4 * t + b : 4 * t + b + 1, :] for b in range(4)], axis=1)
        turned = pltpu.roll(jnp.broadcast_to(row, (128, 512)), 0, 1, stride=1, stride_axis=0)
        return jnp.concatenate(
            [
                jnp.concatenate([turned[:, 256 + 128 * (k - s) :][:, :128] for k in range(2)], axis=1)
                for s in range(2)
            ],
            axis=0,
        )

    late0 = late(0)
    gram = (early(0) + dot(late0, late0, 1, 1)) / count
    eye = jnp.where(iota((128, 128), 0) == iota((128, 128), 1), 1.0, 0.0).astype(jnp.float32)
    work[:, :128] = gram[:128, :128]
    work[:, 128:] = eye
    factor_inverse(work, 128)
    first = work[:, 128:]
    below = dot(gram[128:, :128], first, 1, 1)
    work[:, :128] = gram[128:, 128:] - dot(below, below, 1, 1)
    work[:, 128:] = eye
    factor_inverse(work, 128)
    second = work[:, 128:]
    low[:128, :128] = first
    low[:128, 128:] = zero
    low[128:, :128] = -dot(second, dot(below, first))
    low[128:, 128:] = second
    inverse = low[...]

    basis = dot(toeplitz(0), inverse, 1, 1)
    for t in range(2):
        cross = (early(1 + t) + dot(late0, late(1 + t), 1, 1)) / count
        coupled = dot(inverse, cross)
        coup_ref[:, 256 * t : 256 * t + 256] = coupled
        over_ref[:, 256 * t : 256 * t + 256] = toeplitz(1 + t) - dot(basis, coupled)

    @pl.when(lax.axis_index("col") == 0)
    def _():
        over_ref[:, :WIDE] = basis


def remainder(sums, ext, tail, count):
    rows = ext.shape[1] - TAPS
    f32 = jnp.float32
    return pl.pallas_call(
        functools.partial(remainder_kernel, count),
        name="remainder",
        out_shape=(jax.ShapeDtypeStruct((rows, 512), f32), jax.ShapeDtypeStruct((WIDE, 512), f32)),
        in_specs=[VM, VM, VM],
        out_specs=(VM, VM),
        scratch_shapes=[pltpu.VMEM((128, 256), f32), pltpu.VMEM((256, 256), f32)],
    )(sums, ext, tail)


def solution(mesh):
    slabs, cols = mesh.shape["row"] // SLAB, mesh.shape["col"]

    def body(traces):
        count = traces.shape[1] * slabs * SLAB
        sums, ext, tail = lag_sums(traces, slabs, cols)
        return remainder(sums, ext, tail, count)

    return jax.shard_map(
        body,
        mesh=mesh,
        in_specs=(P("col", "row"),),
        out_specs=(P("row", "col"), P(None, "col")),
        check_vma=False,
    )
```

time: 658 us -> 58.9 us (0.09)
  waiting for transfers between devices: 527 us -> 0 us
  Pallas kernels: 0 us -> 58 us
  other arithmetic: 50.2 us -> 0 us
  local copies, waits for them, and re-layouts: 35.8 us -> 0 us
  between operations: 14.3 us -> 0.64 us
  matrix products: 13.6 us -> 0 us
  blocking collectives: 12.8 us -> 0 us
    psum x2 -> x0, waiting for transfers between devices: 526 us -> none  [body(): ahead_sum, cross_sum = lax.psum((ahead_local, cross_local), 'row')]
    pallas_call x0 -> x2, Pallas kernels: none -> 58 us  [the longest x1 34.1 us: lag_sums(): pl.pallas_call(functools.partial(lag_kernel, slabs, cols), name='lag_sums...]
    another operation x10 -> x0, other arithmetic: 45.9 us -> none  [the longest x6 25 us: triangle_inverse(): factor_low = jnp.linalg.cholesky(gram_part)]
    slice x6 -> x0, local copies, waits for them, and re-layouts: 19.5 us -> none  [the longest x2 16.5 us: hankel_piece(): jnp.tile(flipped, (1, row_count + 1))[:, :row_count * (length + 1)]]
    dot_general x12 -> x0, matrix products: 13 us -> none  [the longest x2 3.07 us: body(): jnp.dot(basis_part, cross_coupled, precision=highest)]
    psum x1 -> x0, blocking collectives: 12.8 us -> none  [from_root(): return lax.psum(kept, axis)]
    reshape x3 -> x0, local copies, waits for them, and re-layouts: 9.77 us -> none  [the longest x2 9.64 us: hankel_piece(): repeated.reshape(segment.shape[0], row_count, length + 1)[:, :, :col_count]]
  transfers between devices with their start and end apart: 3 -> 0, of which waited for: 3 -> 0; matrix products, arithmetic and copies ran while one was open for 0% -> 0% of each run, Pallas kernels for 0% -> 0%
where the time goes in v1:
time: 58.9 us; the launch traced here: 58.7 us
  Pallas kernels  58 us (98%)
  between operations  0.64 us (1%)
    pallas_call x1, Pallas kernels, lag_sums(): pl.pallas_call(functools.partial(lag_kernel, slabs, cols), name='lag_sums...  34.1 us
    pallas_call x1, Pallas kernels, remainder(): pl.pallas_call(functools.partial(remainder_kernel, count), name='remainde...  23.9 us

profile of v1, /device:TPU:2, one launch (start us, length us, event | category | flops | bytes accessed | tf_op | source)
XLA Modules:
  0.0 58.7 jit_solution(11412392408634874282)
XLA Ops:
  0.6 34.1 %lag_sums.1 = (f32[12,128]{1,0:T(8,128)}, f32[3,768]{1,0:T(4,128)}, f32[3,256]{1,0:T(4,128)}) custom-call(f32[2,512]{1,0:T(2,128)} %x_ref.1), custom_call_target="tpu_custom_call" | custom-call | tf_op jit(solution)/shard_map/lag_sums/pallas_call | solution.py:308
  34.8 23.9 %remainder.1 = (f32[512,512]{1,0:T(8,128)}, f32[256,512]{1,0:T(8,128)}) custom-call(f32[12,128]{1,0:T(8,128)} %get-tuple-element.5.sums_ref, f32[3,768]{1,0:T(4,128)} %get-tuple-element.6.ext_ref, f32[3,256]{1,0:T(4,128)} %get-tuple-element.7.tail_ref), custom_call_target="tpu_custom_call" | custom-call | tf_op jit(solution)/shard_map/remainder/pallas_call | solution.py:442

commit v2 on v1

--- a/solution.py
+++ b/solution.py
@@ -335,105 +335,268 @@
             dma((2, slabs)), dma((2,)),
             dma((slabs,)), dma((slabs,)),
         ],
-        compiler_params=pltpu.CompilerParams(collective_id=0, has_side_effects=True),
+        compiler_params=pltpu.CompilerParams(
+            collective_id=0, has_side_effects=True, vmem_limit_bytes=8 * 2**20
+        ),
     )(traces)
 
 
-def factor_inverse(work, size):
+def split(x):
+    high = x.astype(jnp.bfloat16)
+    return high, (x - high.astype(jnp.float32)).astype(jnp.bfloat16)
+
+
+def dot3(a, b, nt=False):
+    (ah, al), (bh, bl) = a, b
+    left = jnp.concatenate([ah, al, ah], axis=1)
+    right = jnp.concatenate([bh, bh, bl], axis=1 if nt else 0)
+    return lax.dot_general(
+        left, right, (((1,), (1 if nt else 0,)), ((), ())), preferred_element_type=jnp.float32
+    )
+
+
+def tree(terms):
+    while len(terms) > 1:
+        terms = [terms[i] + terms[i + 1] if i + 1 < len(terms) else terms[i] for i in range(0, len(terms), 2)]
+    return terms[0]
+
+
+def pick(v, j):
+    return jnp.broadcast_to(v[j : j + 1], (8, 128))
+
+
+def eliminate(cols):
     sub = iota((8, 128), 0)
-    lane = iota((8, size), 1)
-    for k in range(size // 8):
-        here = work[8 * k : 8 * k + 8, :]
-        cols = [jnp.broadcast_to(here[:, 8 * k + j : 8 * k + j + 1], (8, 128)) for j in range(8)]
-        invs = [jnp.where(sub == j, 1.0, 0.0).astype(jnp.float32) for j in range(8)]
-        for j in range(8):
-            scale = lax.rsqrt(jnp.broadcast_to(cols[j][j : j + 1], (8, 128)))
-            below = jnp.where(sub > j, cols[j] * scale, 0.0)
-            for m in range(j + 1, 8):
-                cols[m] = cols[m] - below * (jnp.broadcast_to(cols[m][j : j + 1], (8, 128)) * scale)
-            for m in range(j + 1):
-                piv = jnp.broadcast_to(invs[m][j : j + 1], (8, 128)) * scale
-                invs[m] = jnp.where(sub == j, piv, invs[m] - below * piv)
-        done = None
-        for m in range(8):
-            wide = jnp.concatenate([invs[m]] * (2 * size // 128), axis=1) * jnp.broadcast_to(here[m : m + 1, :], (8, 2 * size))
-            done = wide if done is None else done + wide
-        work[8 * k : 8 * k + 8, :] = done
-        if 8 * k + 8 < size:
-            left = jnp.where(lane > 8 * k + 7, done[:, :size], 0.0)
-            change = dot(left, done, 0, 0)
-            work[8 * k + 8 :, :] = work[8 * k + 8 :, :] - change[8 * k + 8 :, :]
-
-
-def remainder_kernel(count, sums_ref, ext_ref, tail_ref, over_ref, coup_ref, work, low):
-    flip = anti_identity()
+    cols = list(cols)
+    invs = [jnp.where(sub == j, 1.0, 0.0).astype(jnp.float32) for j in range(8)]
+    scales = None
+    for j in range(8):
+        scale = lax.rsqrt(pick(cols[j], j))
+        scales = scale if scales is None else jnp.where(sub == j, scale, scales)
+        if j == 7:
+            break
+        below = jnp.where(sub > j, cols[j], 0.0)
+        square = scale * scale
+        ratio = below * square
+        cols[j + 1] = cols[j + 1] - (below * pick(cols[j + 1], j)) * square
+        for m in range(j + 2, 8):
+            cols[m] = cols[m] - ratio * pick(cols[m], j)
+        for m in range(j):
+            invs[m] = invs[m] - ratio * pick(invs[m], j)
+        invs[j] = invs[j] - ratio
+    return [v * scales for v in invs]
+
+
+def thirds(x):
+    high = x.astype(jnp.bfloat16).astype(jnp.float32)
+    rest = x - high
+    mid = rest.astype(jnp.bfloat16).astype(jnp.float32)
+    return high, mid, rest - mid
+
+
+def outer6(a, b):
+    (ah, am, al), (bh, bm, bl) = a, b
+    left = jnp.concatenate([ah, ah, am, am, ah, al], axis=0).astype(jnp.bfloat16)
+    right = jnp.concatenate([bh, bm, bh, bm, bl, bh], axis=0).astype(jnp.bfloat16)
+    return lax.dot_general(left, right, (((0,), (0,)), ((), ())), preferred_element_type=jnp.float32)
+
+
+def factor_inverse(blocks, beside):
+    count = len(blocks)
+    beside = list(beside)
+    due = [i * (count - 1) // len(beside) for i in range(len(beside))]
+    mat = list(blocks)
+    lane, sub = iota((8, 128), 1), iota((8, 128), 0)
+    out = [jnp.where(lane == sub + 8 * i, 1.0, 0.0).astype(jnp.float32) for i in range(count)]
+
+    def column(i, c):
+        return jnp.broadcast_to(mat[i][:, c : c + 1], (8, 128))
+
+    def apply(vectors, block):
+        return tree([vectors[m] * pick(block, m) for m in range(8)])
+
+    cols = [column(0, m) for m in range(8)]
+    for k in range(count):
+        invs = eliminate(cols)
+        out[k] = apply(invs, out[k])
+        if k + 1 == count:
+            break
+        done = apply(invs, mat[k])
+        nxt = k + 1
+        by = [column(nxt, 8 * k + m) for m in range(8)]
+        factor = [tree([by[m] * pick(invs[m], j) for m in range(j + 1)]) for j in range(8)]
+        if True:
+            old = [column(nxt, 8 * nxt + m) for m in range(8)]
+            cols = [old[m] - tree([factor[j] * pick(factor[j], m) for j in range(8)]) for m in range(8)]
+        mat[nxt] = mat[nxt] - apply(factor, done)
+        out[nxt] = out[nxt] - apply(factor, out[k])
+        if not True:
+            cols = [column(nxt, 8 * nxt + m) for m in range(8)]
+        if nxt + 1 < count:
+            both = thirds(jnp.concatenate([done, out[k]], axis=1))
+            change = outer6([part[:, :128] for part in both], both)
+            for i in range(nxt + 1, count):
+                mat[i] = mat[i] - change[8 * i : 8 * i + 8, :128]
+                out[i] = out[i] - change[8 * i : 8 * i + 8, 128:]
+        for when, piece in zip(due, beside):
+            if when == k:
+                piece()
+    return out
+
+
+def dot6(a, b):
+    (ah, am, al), (bh, bm, bl) = ([v.astype(jnp.bfloat16) for v in x] for x in (a, b))
+
+    def part(u, v):
+        return lax.dot_general(u, v, (((1,), (1,)), ((), ())), preferred_element_type=jnp.float32)
+
+    def beside(u, v):
+        return jnp.concatenate([u, v], axis=1)
+
+    size = bh.shape[0]
+    main = part(beside(ah, am), jnp.concatenate([beside(bh, bm), beside(bm, bh)], axis=0))
+    return main[:, :size] + (main[:, size:] + part(beside(ah, al), beside(bl, bh)))
+
+
+def remainder_kernel(
+    count, sums_ref, ext_ref, tail_ref, over_ref, coup_ref, panel_ref, panel2_ref, basis_ref, cross_ref, flip_ref
+):
     blocks = (ext_ref.shape[1]) // 128
-    ext = jnp.concatenate(
-        [ext_ref[t : t + 1, 128 * b : 128 * b + 128] for t in range(3) for b in range(blocks)], axis=0
-    )
-    flipped = dot(ext, flip)
-
-    def toeplitz(t):
-        row = jnp.concatenate(
-            [flipped[blocks * t + b : blocks * t + b + 1] for b in reversed(range(blocks))], axis=1
-        )
-        turned = pltpu.roll(jnp.broadcast_to(row, (128, 128 * blocks)), 1, 1, stride=1, stride_axis=0)
-        return jnp.concatenate(
-            [
-                jnp.concatenate([turned[:, 512 - 128 * (s - k) :][:, :128] for k in range(2)], axis=1)
-                for s in range(blocks - 2)
-            ],
-            axis=0,
-        )
-
-    zero = jnp.zeros((128, 128), jnp.float32)
+    steps = blocks - 2
+    parts = 128 * steps // 512
 
     def late(t):
         tail = jnp.where(iota((1, TAPS), 1) == 0, 0.0, tail_ref[t : t + 1, :])
         row = jnp.concatenate([jnp.zeros((1, 128), jnp.float32), tail], axis=1)
         turned = pltpu.roll(jnp.broadcast_to(row, (128, 384)), 0, 1, stride=1, stride_axis=0)
-        top = jnp.concatenate([turned[:, 128:256], turned[:, 256:384]], axis=1)
-        return jnp.concatenate([top, jnp.concatenate([zero, turned[:, 128:256]], axis=1)], axis=0)
+        return turned[:, 128:256], turned[:, 256:384]
 
     def early(t):
         row = jnp.concatenate([sums_ref[4 * t + b : 4 * t + b + 1, :] for b in range(4)], axis=1)
         turned = pltpu.roll(jnp.broadcast_to(row, (128, 512)), 0, 1, stride=1, stride_axis=0)
-        return jnp.concatenate(
-            [
-                jnp.concatenate([turned[:, 256 + 128 * (k - s) :][:, :128] for k in range(2)], axis=1)
-                for s in range(2)
-            ],
-            axis=0,
+        return turned[:, 256:512], turned[:, 128:384]
+
+    near0, far0 = late(0)
+    gram_top, gram_low = early(0)
+    near6, far6 = thirds(near0), thirds(far0)
+    near_near = dot6(near6, near6)
+    gram11 = (gram_top[:, :128] + (near_near + dot6(far6, far6))) / count
+    got = {}
+
+    def gram_rest():
+        got["gram21"] = thirds((gram_low[:, :128] + dot6(near6, far6)) / count)
+        got["gram22"] = (gram_low[:, 128:] + near_near) / count
+
+    def turn_around():
+        ext = jnp.concatenate(
+            [ext_ref[t : t + 1, 128 * b : 128 * b + 128] for t in range(3) for b in range(blocks)], axis=0
         )
-
-    late0 = late(0)
-    gram = (early(0) + dot(late0, late0, 1, 1)) / count
-    eye = jnp.where(iota((128, 128), 0) == iota((128, 128), 1), 1.0, 0.0).astype(jnp.float32)
-    work[:, :128] = gram[:128, :128]
-    work[:, 128:] = eye
-    factor_inverse(work, 128)
-    first = work[:, 128:]
-    below = dot(gram[128:, :128], first, 1, 1)
-    work[:, :128] = gram[128:, 128:] - dot(below, below, 1, 1)
-    work[:, 128:] = eye
-    factor_inverse(work, 128)
-    second = work[:, 128:]
-    low[:128, :128] = first
-    low[:128, 128:] = zero
-    low[128:, :128] = -dot(second, dot(below, first))
-    low[128:, 128:] = second
-    inverse = low[...]
-
-    basis = dot(toeplitz(0), inverse, 1, 1)
-    for t in range(2):
-        cross = (early(1 + t) + dot(late0, late(1 + t), 1, 1)) / count
-        coupled = dot(inverse, cross)
-        coup_ref[:, 256 * t : 256 * t + 256] = coupled
-        over_ref[:, 256 * t : 256 * t + 256] = toeplitz(1 + t) - dot(basis, coupled)
+        flip_ref[0 : 3 * blocks, :] = dot(ext, anti_identity())
+
+    def toeplitz(t):
+        def piece():
+            row = jnp.concatenate(
+                [flip_ref[blocks * t + b : blocks * t + b + 1, :] for b in reversed(range(blocks))], axis=1
+            )
+            turned = pltpu.roll(jnp.broadcast_to(row, (128, 128 * blocks)), 1, 1, stride=1, stride_axis=0)
+            for k in range(2):
+                for s in range(steps):
+                    rows, at = slice(128 * s, 128 * s + 128), 128 * k
+                    block = turned[:, 512 + 128 * (k - s) : 640 + 128 * (k - s)]
+                    if t == 0:
+                        panel_ref[rows, at : at + 128] = block
+                    else:
+                        over_ref[rows, 256 * (t - 1) + at : 256 * (t - 1) + at + 128] = block
+
+        return piece
+
+    def cross(t):
+        def piece():
+            near, far = late(t)
+            top, low = early(t)
+            near_a, far_a, near_c, far_c = split(near0), split(far0), split(near), split(far)
+            same = dot3(near_a, near_c, True)
+            at = 256 * (t - 1)
+            cross_ref[:128, at : at + 128] = (top[:, :128] + (same + dot3(far_a, far_c, True))) / count
+            cross_ref[:128, at + 128 : at + 256] = (top[:, 128:] + dot3(far_a, near_c, True)) / count
+            cross_ref[128:, at : at + 128] = (low[:, :128] + dot3(near_a, far_c, True)) / count
+            cross_ref[128:, at + 128 : at + 256] = (low[:, 128:] + same) / count
+
+        return piece
+
+    first = jnp.concatenate(
+        factor_inverse(
+            [gram11[8 * i : 8 * i + 8] for i in range(16)],
+            [gram_rest, turn_around] + [toeplitz(t) for t in range(3)] + [cross(1 + t) for t in range(2)],
+        ),
+        axis=0,
+    )
+    below = dot6(got["gram21"], thirds(first))
+    below6 = thirds(below)
+    schur = got["gram22"] - dot6(below6, below6)
+    first2, below2 = split(first), split(below)
+
+    def wide(i):
+        return slice(256 * i, 256 * i + 256)
+
+    def couple(i):
+        def piece():
+            coup_ref[:128, wide(i)] = dot3(first2, split(cross_ref[:128, wide(i)]))
+
+        return piece
+
+    def couple_rest(i):
+        def piece():
+            cross_ref[128:, wide(i)] = cross_ref[128:, wide(i)] - dot3(below2, split(coup_ref[:128, wide(i)]))
+
+        return piece
+
+    def upper(s):
+        return slice(512 * s, 512 * s + 512)
+
+    def orthogonalize(s):
+        def piece():
+            basis_ref[upper(s), :] = dot3(split(panel_ref[upper(s), :128]), first2, True)
+
+        return piece
+
+    def orthogonalize_rest(s):
+        def piece():
+            panel2_ref[upper(s), :] = panel_ref[upper(s), 128:] - dot3(split(basis_ref[upper(s), :]), below2, True)
+
+        return piece
+
+    def project(s, i):
+        def piece():
+            change = dot3(split(basis_ref[upper(s), :]), split(coup_ref[:128, wide(i)]))
+            over_ref[upper(s), wide(i)] = over_ref[upper(s), wide(i)] - change
+
+        return piece
+
+    second = jnp.concatenate(
+        factor_inverse(
+            [schur[8 * i : 8 * i + 8] for i in range(16)],
+            [couple(i) for i in range(2)]
+            + [orthogonalize(s) for s in range(parts)]
+            + [project(s, i) for i in range(2) for s in range(parts)]
+            + [couple_rest(i) for i in range(2)]
+            + [orthogonalize_rest(s) for s in range(parts)],
+        ),
+        axis=0,
+    )
+    second2 = split(second)
+    basis2 = dot3(split(panel2_ref[...]), second2, True)
+    panel2_ref[...] = basis2
+    basis2s = split(basis2)
+    for i in range(2):
+        coup2 = dot3(second2, split(cross_ref[128:, wide(i)]))
+        coup_ref[128:, wide(i)] = coup2
+        over_ref[:, wide(i)] = over_ref[:, wide(i)] - dot3(basis2s, split(coup2))
 
     @pl.when(lax.axis_index("col") == 0)
     def _():
-        over_ref[:, :WIDE] = basis
+        over_ref[:, :128] = basis_ref[...]
+        over_ref[:, 128:WIDE] = panel2_ref[...]
 
 
 def remainder(sums, ext, tail, count):
@@ -445,7 +608,14 @@
         out_shape=(jax.ShapeDtypeStruct((rows, 512), f32), jax.ShapeDtypeStruct((WIDE, 512), f32)),
         in_specs=[VM, VM, VM],
         out_specs=(VM, VM),
-        scratch_shapes=[pltpu.VMEM((128, 256), f32), pltpu.VMEM((256, 256), f32)],
+        scratch_shapes=[
+            pltpu.VMEM((rows, WIDE), f32),
+            pltpu.VMEM((rows, 128), f32),
+            pltpu.VMEM((rows, 128), f32),
+            pltpu.VMEM((WIDE, 512), f32),
+            pltpu.VMEM((24, 128), f32),
+        ],
+        compiler_params=pltpu.CompilerParams(vmem_limit_bytes=24 * 2**20),
     )(sums, ext, tail)
 
 

time: 58.9 us -> 43.4 us (0.74)
  Pallas kernels: 58 us -> 41.9 us
  local copies, waits for them, and re-layouts: 0 us -> 0.68 us
    pallas_call x1, Pallas kernels: 23.9 us -> 8.96 us  [remainder(): pl.pallas_call(functools.partial(remainder_kernel, count), name='remainde...]
    pallas_call x1, Pallas kernels: 34.1 us -> 32.9 us  [lag_sums(): pl.pallas_call(functools.partial(lag_kernel, slabs, cols), name='lag_sums...]
    unnamed x0 -> x2, local copies, waits for them, and re-layouts: none -> 0.68 us
where the time goes in v2:
time: 43.4 us; the launch traced here: 43.2 us
  Pallas kernels  41.9 us (97%)
  local copies, waits for them, and re-layouts  0.68 us (2%)
  between operations  0.65 us (1%)
    pallas_call x1, Pallas kernels, lag_sums(): pl.pallas_call(functools.partial(lag_kernel, slabs, cols), name='lag_sums...  32.9 us
    pallas_call x1, Pallas kernels, remainder(): pl.pallas_call(functools.partial(remainder_kernel, count), name='remainde...  8.96 us

profile of v2, /device:TPU:2, one launch (start us, length us, event | category | flops | bytes accessed | tf_op | source)
XLA Modules:
  0.0 43.2 jit_solution(4608281135985901879)
XLA Ops:
  0.6 0.0 copy-start
  0.6 0.7 %copy-done = f32[2,512]{1,0:T(2,128)S(1)} copy-done((f32[2,512]{1,0:T(2,128)S(1)}, f32[2,512]{1,0:T(2,128)}, u32[]{:S(2)}) %copy-start) | copy-done | bytes 4120
  1.3 32.9 %lag_sums.1 = (f32[12,128]{1,0:T(8,128)S(1)}, f32[3,768]{1,0:T(4,128)S(1)}, f32[3,256]{1,0:T(4,128)S(1)}) custom-call(f32[2,512]{1,0:T(2,128)S(1)} %copy-done), custom_call_target="tpu_custom_call" | custom-call | tf_op jit(solution)/shard_map/lag_sums/pallas_call | solution.py:308
  34.3 9.0 %remainder.1 = (f32[512,512]{1,0:T(8,128)}, f32[256,512]{1,0:T(8,128)}) custom-call(f32[12,128]{1,0:T(8,128)S(1)} %get-tuple-element.5.sums_ref, f32[3,768]{1,0:T(4,128)S(1)} %get-tuple-element.6.ext_ref, f32[3,256]{1,0:T(4,128)S(1)} %get-tuple-element.7.tail_ref), custom_call_target="tpu_custom_call" | custom-call | tf_op jit(solution)/shard_map/remainder/pallas_call | solution.py:605
Async XLA Ops:
  0.6 0.7 %copy-start = (f32[2,512]{1,0:T(2,128)S(1)}, f32[2,512]{1,0:T(2,128)}, u32[]{:S(2)}) copy-start(f32[2,512]{1,0:T(2,128)} %x_ref.1) | copy-start | bytes 12292

commit v3 on v2

--- a/solution.py
+++ b/solution.py
@@ -32,20 +32,22 @@
 def lag_kernel(
     slabs, cols,
     x_ref, sums_ref, ext_ref, tail_ref,
-    own0, slab0, slabc, before0, after0, beforec, tail0, tailc, lags,
+    mine, own0, slab0, slabc, before0, after0, beforec, late0, latec, lags,
     local_sem, send_x, recv_x, send_0, recv_0, send_hc, recv_hc,
-    send_s0, recv_s0, send_hb, recv_hb, send_ha, recv_ha, send_t, recv_t, send_l, recv_l,
+    send_s0, recv_s0, send_hb, recv_hb, send_ha, recv_ha, send_t, recv_t, send_l, recv_l, hello,
 ):
     row, col = lax.axis_index("row"), lax.axis_index("col")
     z, y = row // SLAB, row % SLAB
-    rows = x_ref.shape[1]
-    cut = rows - TAPS
+    per = x_ref.shape[1] // 128
     first, last = y == 0, y == SLAB - 1
     has_before, has_after = z > 0, z < slabs - 1
     in_tail = z == slabs - 1
 
     def at(zz, yy, cc):
         return (zz * SLAB + yy, cc)
+
+    def around(k):
+        return at((z + k + slabs) % slabs, y, col)
 
     def remote(src, dst, send, recv, where):
         return pltpu.make_async_remote_copy(
@@ -57,45 +59,44 @@
     def greet(where):
         pl.semaphore_signal(barrier, inc=1, device_id=where, device_id_type=MESH)
 
-    @pl.loop(1, slabs)
-    def _(k):
-        greet(at((z + k) % slabs, y, col))
+    greet(around(1))
+    greet(around(-1))
+
+    @pl.when(last & has_after)
+    def _():
+        for k in range(SLAB):
+            greet(at(z + 1, k, col))
+
+    @pl.when(first & has_before)
+    def _():
+        for k in range(SLAB):
+            greet(at(z - 1, k, col))
+
+    @pl.when(has_before)
+    def _():
+        greet(at(z - 1, SLAB - 1, col))
+
+    @pl.when(has_after)
+    def _():
+        greet(at(z + 1, 0, col))
+
+    @pl.when(col == 0)
+    def _():
+        for k in range(1, cols):
+            greet(at(z, y, k))
+
+    @pl.when(col != 0)
+    def _():
+        greet(at(z, y, 0))
 
     for k in range(1, SLAB):
         greet(at(z, (y + k) % SLAB, col))
 
-    @pl.when(col == 0)
-    def _():
-        for k in range(1, cols):
-            greet(at(z, y, k))
-
-    @pl.when(col != 0)
-    def _():
-        greet(at(z, y, 0))
-
-    @pl.when(last & has_after)
-    def _():
-        for k in range(SLAB):
-            greet(at(z + 1, k, col))
-
-    @pl.when(first & has_before)
-    def _():
-        for k in range(SLAB):
-            greet(at(z - 1, k, col))
-
-    @pl.when(has_before)
-    def _():
-        greet(at(z - 1, SLAB - 1, col))
-
-    @pl.when(has_after)
-    def _():
-        greet(at(z + 1, 0, col))
-
     def yes(flag):
         return jnp.where(flag, 1, 0)
 
     expected = (
-        slabs - 1 + SLAB - 1 + 1 + (cols - 2) * yes(col == 0)
+        2 + SLAB - 1 + yes(col != 0) + (cols - 1) * yes(col == 0)
         + SLAB * yes(last & has_after) + SLAB * yes(first & has_before)
         + yes(has_before) + yes(has_after)
     )
@@ -109,186 +110,192 @@
     def _():
         after0[...] = jnp.zeros_like(after0)
 
-    keep_c = pltpu.make_async_copy(x_ref, slabc.at[y], local_sem.at[0])
-    keep_c.start()
+    plain = jnp.concatenate(
+        [x_ref[t : t + 1, 128 * b : 128 * b + 128] for t in range(2) for b in range(per)], axis=0
+    )
+    turned = dot(plain, anti_identity())
+    mine[...] = turned
+    slabc[y] = turned
+
+    @pl.when(col == 0)
+    def _():
+        own0[:per, :] = plain[:per]
+        own0[per:, :] = turned[:per]
+
     pl.semaphore_wait(barrier, expected)
 
     @pl.when(col == 0)
     def _():
         for k in range(1, cols):
-            remote(x_ref.at[0:1, :], own0.at[0:1, :], send_0.at[k], recv_0.at[0], at(z, y, k)).start()
-        own = pltpu.make_async_copy(x_ref.at[0:1, :], own0.at[0:1, :], local_sem.at[1])
-        own.start()
-        own.wait()
+            remote(own0, own0, send_0.at[k], recv_0.at[0], at(z, y, k)).start()
 
     for k in range(1, SLAB):
-        remote(x_ref, slabc.at[y], send_x.at[k], recv_x.at[y], at(z, (y + k) % SLAB, col)).start()
+        remote(mine, slabc.at[y], send_x.at[k], recv_x.at[y], at(z, (y + k) % SLAB, col)).start()
 
     @pl.when(last & has_after)
     def _():
-        remote(x_ref.at[:, cut:], beforec, send_hc.at[0], recv_hc.at[0], at(z + 1, 0, col)).start()
+        remote(mine, beforec, send_hc.at[0], recv_hc.at[0], at(z + 1, 0, col)).start()
+
+    reach = [r for r in (1, 2, 4, 8, 16) if 4 * r <= slabs]
+
+    def tell(i):
+        for k in (reach[i], -reach[i]):
+            pl.semaphore_signal(hello.at[i], inc=1, device_id=around(k), device_id_type=MESH)
+
+    if reach:
+        tell(0)
+    if len(reach) > 1:
+        pl.semaphore_wait(hello.at[0], 2)
+        tell(1)
 
     @pl.when(col != 0)
     def _():
-        remote(x_ref.at[0:1, :], own0.at[0:1, :], send_0.at[0], recv_0.at[0], at(z, y, 0)).wait_recv()
-
-    keep_0 = pltpu.make_async_copy(own0.at[0:1, :], slab0.at[y, 0:1, :], local_sem.at[2])
+        remote(own0, own0, send_0.at[0], recv_0.at[0], at(z, y, 0)).wait_recv()
+
+    keep_0 = pltpu.make_async_copy(own0, slab0.at[y], local_sem.at[0])
     keep_0.start()
     for k in range(1, SLAB):
-        remote(
-            own0.at[0:1, :], slab0.at[y, 0:1, :], send_s0.at[k], recv_s0.at[y], at(z, (y + k) % SLAB, col)
-        ).start()
+        remote(own0, slab0.at[y], send_s0.at[k], recv_s0.at[y], at(z, (y + k) % SLAB, col)).start()
 
     @pl.when(last & has_after)
     def _():
         for k in range(SLAB):
-            remote(
-                own0.at[0:1, cut:], before0.at[0:1, :], send_hb.at[k], recv_hb.at[0], at(z + 1, k, col)
-            ).start()
+            remote(own0, before0, send_hb.at[k], recv_hb.at[0], at(z + 1, k, col)).start()
 
     @pl.when(first & has_before)
     def _():
         for k in range(SLAB):
-            remote(
-                own0.at[0:1, :TAPS], after0.at[0:1, :], send_ha.at[k], recv_ha.at[0], at(z - 1, k, col)
-            ).start()
-
-    keep_c.wait()
+            remote(own0.at[0:2], after0, send_ha.at[k], recv_ha.at[0], at(z - 1, k, col)).start()
+
+    for i in range(2, len(reach)):
+        pl.semaphore_wait(hello.at[i - 1], 2)
+        tell(i)
+
     keep_0.wait()
     for k in range(1, SLAB):
         other = (y + k) % SLAB
-        remote(x_ref, slabc.at[other], send_x.at[k], recv_x.at[other], at(z, other, col)).wait_recv()
-        remote(
-            own0.at[0:1, :], slab0.at[other, 0:1, :], send_s0.at[k], recv_s0.at[other], at(z, other, col)
-        ).wait_recv()
+        remote(mine, slabc.at[other], send_x.at[k], recv_x.at[other], at(z, other, col)).wait_recv()
+        remote(own0, slab0.at[other], send_s0.at[k], recv_s0.at[other], at(z, other, col)).wait_recv()
 
     @pl.when(has_before)
     def _():
-        remote(own0.at[0:1, cut:], before0.at[0:1, :], send_hb.at[0], recv_hb.at[0], at(z, y, col)).wait_recv()
+        remote(own0, before0, send_hb.at[0], recv_hb.at[0], at(z, y, col)).wait_recv()
 
     @pl.when(has_after)
     def _():
-        remote(own0.at[0:1, :TAPS], after0.at[0:1, :], send_ha.at[0], recv_ha.at[0], at(z, y, col)).wait_recv()
-
-    def tails(k):
-        where = at((z + k) % slabs, y, col)
-        return (
-            remote(slab0.at[SLAB - 1, 0:1, cut:], tail0.at[0:1, :], send_t.at[0, k], recv_t.at[0], where),
-            remote(slabc.at[SLAB - 1, :, cut:], tailc, send_t.at[1, k], recv_t.at[1], where),
-        )
-
-    @pl.when(in_tail)
-    def _():
-        @pl.loop(1, slabs)
-        def _(k):
-            for copy in tails(k):
-                copy.start()
-
-        tail0[0:1, :] = slab0[SLAB - 1, 0:1, cut:]
-        tailc[...] = slabc[SLAB - 1, :, cut:]
-
-    per = rows // 128
+        remote(own0.at[0:2], after0, send_ha.at[0], recv_ha.at[0], at(z, y, col)).wait_recv()
+
     count = SLAB * per
-    block0 = [before0[0:1, 0:128], before0[0:1, 128:256]]
-    for j in range(SLAB):
-        block0 += [slab0[j, 0:1, 128 * b : 128 * b + 128] for b in range(per)]
-    block0 += [after0[0:1, 0:128], after0[0:1, 128:256]]
-    ext0 = jnp.concatenate(block0, axis=0)
+    ext0 = jnp.concatenate([before0[per - 2 : per, :]] + [slab0[j, :per, :] for j in range(SLAB)] + [after0[...]], axis=0)
     wide0 = jnp.concatenate([ext0[k : k + count] for k in range(5)], axis=1)
     place = iota((count, 640), 0) * 128 + iota((count, 640), 1) - 256
     late = count * 128 - (TAPS - 1)
     wide0_early = jnp.where(in_tail & (place >= late), 0.0, wide0)
     right = jnp.concatenate([wide0, wide0_early[count - 8 :]], axis=0)
-    flip = anti_identity()
-    at_late = in_tail & (iota((count, 128), 0) * 128 + iota((count, 128), 1) >= late)
+    at_late = in_tail & (iota((count, 128), 0) * 128 + 127 - iota((count, 128), 1) >= late)
     lefts = []
     for t in range(3):
         if t == 0:
-            mine = ext0[2 : 2 + count]
+            group = jnp.concatenate([slab0[j, per:, :] for j in range(SLAB)], axis=0)
         else:
-            mine = jnp.concatenate(
-                [slabc[j, t - 1 : t, 128 * b : 128 * b + 128] for j in range(SLAB) for b in range(per)], axis=0
-            )
-        lefts += [jnp.where(at_late, 0.0, mine), jnp.where(at_late, mine, 0.0)[count - 8 :]]
-    flipped = dot(jnp.concatenate(lefts, axis=0), flip)
-    deep = count + 8
+            group = jnp.concatenate([slabc[j, per * (t - 1) : per * t, :] for j in range(SLAB)], axis=0)
+        lefts.append(
+            jnp.concatenate([jnp.where(at_late, 0.0, group), jnp.where(at_late, group, 0.0)[count - 8 :]], axis=0)
+        )
+    table = outer6(thirds(jnp.concatenate(lefts, axis=1)), thirds(right))
     for t in range(3):
-        table = dot(flipped[deep * t : deep * t + deep], right, 0, 0)
-        skewed = pltpu.roll(table, 1, 1, stride=1, stride_axis=0)
+        skewed = pltpu.roll(table[128 * t : 128 * t + 128], 1, 1, stride=1, stride_axis=0)
         summed = jnp.sum(skewed, axis=0, keepdims=True)
         for b in range(4):
             lags[z, 4 * t + b : 4 * t + b + 1, :] = summed[:, 128 + 128 * b : 256 + 128 * b]
 
+    if reach:
+        pl.semaphore_wait(hello.at[len(reach) - 1], 2)
+
     def exchange(k):
-        where = at((z + k) % slabs, y, col)
-        return remote(lags.at[z], lags.at[z], send_l.at[k], recv_l.at[z], where)
-
-    @pl.loop(1, slabs)
+        return remote(lags.at[z], lags.at[z], send_l.at[k], recv_l.at[z], around(k))
+
+    @pl.loop(0, slabs - 1)
     def _(k):
-        exchange(k).start()
-
-    ext_ref[0:1, TAPS:] = own0[0:1, :]
-    ext_ref[1:3, TAPS:] = x_ref[...]
+        exchange(1 + (k + slabs // 2 - 1) % (slabs - 1)).start()
+
+    def tails(k):
+        return (
+            remote(slab0.at[SLAB - 1, per - 2 : per], late0, send_t.at[0, k], recv_t.at[0], around(k)),
+            remote(slabc.at[SLAB - 1, per - 2 : per], latec.at[0], send_t.at[1, k], recv_t.at[1], around(k)),
+            remote(slabc.at[SLAB - 1, 2 * per - 2 :], latec.at[1], send_t.at[2, k], recv_t.at[2], around(k)),
+        )
+
+    @pl.when(in_tail)
+    def _():
+        @pl.loop(1, slabs)
+        def _(k):
+            for copy in tails(k):
+                copy.start()
+
+        late0[...] = slab0[SLAB - 1, per - 2 : per]
+        latec[0] = slabc[SLAB - 1, per - 2 : per]
+        latec[1] = slabc[SLAB - 1, 2 * per - 2 :]
+
+    reach_back = per + 2
+    ext_ref[2:reach_back, :] = own0[per:, :]
+    for t in range(2):
+        ext_ref[reach_back * (t + 1) + 2 : reach_back * (t + 2), :] = mine[per * t : per * t + per, :]
 
     @pl.when(first)
     def _():
-        ext_ref[0:1, :TAPS] = before0[0:1, :]
-
         @pl.when(has_before)
         def _():
-            remote(x_ref.at[:, cut:], beforec, send_hc.at[0], recv_hc.at[0], at(z, y, col)).wait_recv()
-
-        ext_ref[1:3, :TAPS] = beforec[...]
+            remote(mine, beforec, send_hc.at[0], recv_hc.at[0], at(z, y, col)).wait_recv()
+
+        ext_ref[0:2, :] = before0[2 * per - 2 :, :]
+        for t in range(2):
+            ext_ref[reach_back * (t + 1) : reach_back * (t + 1) + 2, :] = beforec[per * t + per - 2 : per * t + per, :]
 
     @pl.when(y > 0)
     def _():
-        ext_ref[0:1, :TAPS] = slab0[(y + SLAB - 1) % SLAB, 0:1, cut:]
-        ext_ref[1:3, :TAPS] = slabc[(y + SLAB - 1) % SLAB, :, cut:]
+        before = (y + SLAB - 1) % SLAB
+        ext_ref[0:2, :] = slab0[before, 2 * per - 2 :, :]
+        for t in range(2):
+            ext_ref[reach_back * (t + 1) : reach_back * (t + 1) + 2, :] = slabc[before, per * t + per - 2 : per * t + per, :]
 
     @pl.when(z < slabs - 1)
     def _():
         for copy in tails(0):
             copy.wait_recv()
 
-    tail_ref[0:1, :] = tail0[0:1, :]
-    tail_ref[1:3, :] = tailc[...]
+    tail_ref[0:2, :] = late0[...]
+    tail_ref[2:4, :] = latec[0]
+    tail_ref[4:6, :] = latec[1]
+    tail_ref[6:8, :] = jnp.zeros((2, 128), jnp.float32)
 
     @pl.loop(1, slabs)
     def _(k):
         other = (z + k) % slabs
         remote(lags.at[other], lags.at[other], send_l.at[k], recv_l.at[other], at(other, y, col)).wait_recv()
 
-    total = lags[0]
-    for k in range(1, slabs):
-        total = total + lags[k]
-    sums_ref[...] = total
+    sums_ref[...] = tree([lags[k] for k in range(slabs)])
 
     @pl.when(col == 0)
     def _():
         for k in range(1, cols):
-            remote(x_ref.at[0:1, :], own0.at[0:1, :], send_0.at[k], recv_0.at[0], at(z, y, k)).wait_send()
+            remote(own0, own0, send_0.at[k], recv_0.at[0], at(z, y, k)).wait_send()
 
     for k in range(1, SLAB):
         other = (y + k) % SLAB
-        remote(x_ref, slabc.at[y], send_x.at[k], recv_x.at[y], at(z, other, col)).wait_send()
-        remote(
-            own0.at[0:1, :], slab0.at[y, 0:1, :], send_s0.at[k], recv_s0.at[y], at(z, other, col)
-        ).wait_send()
+        remote(mine, slabc.at[y], send_x.at[k], recv_x.at[y], at(z, other, col)).wait_send()
+        remote(own0, slab0.at[y], send_s0.at[k], recv_s0.at[y], at(z, other, col)).wait_send()
 
     @pl.when(last & has_after)
     def _():
-        remote(x_ref.at[:, cut:], beforec, send_hc.at[0], recv_hc.at[0], at(z + 1, 0, col)).wait_send()
+        remote(mine, beforec, send_hc.at[0], recv_hc.at[0], at(z + 1, 0, col)).wait_send()
         for k in range(SLAB):
-            remote(
-                own0.at[0:1, cut:], before0.at[0:1, :], send_hb.at[k], recv_hb.at[0], at(z + 1, k, col)
-            ).wait_send()
+            remote(own0, before0, send_hb.at[k], recv_hb.at[0], at(z + 1, k, col)).wait_send()
 
     @pl.when(first & has_before)
     def _():
         for k in range(SLAB):
-            remote(
-                own0.at[0:1, :TAPS], after0.at[0:1, :], send_ha.at[k], recv_ha.at[0], at(z - 1, k, col)
-            ).wait_send()
+            remote(own0.at[0:2], after0, send_ha.at[k], recv_ha.at[0], at(z - 1, k, col)).wait_send()
 
     @pl.when(in_tail)
     def _():
@@ -303,37 +310,39 @@
 
 
 def lag_sums(traces, slabs, cols):
-    rows = traces.shape[1]
+    per = traces.shape[1] // 128
     f32, dma = jnp.float32, pltpu.SemaphoreType.DMA
     return pl.pallas_call(
         functools.partial(lag_kernel, slabs, cols),
         name="lag_sums",
         out_shape=(
             jax.ShapeDtypeStruct((12, 128), f32),
-            jax.ShapeDtypeStruct((3, rows + TAPS), f32),
-            jax.ShapeDtypeStruct((3, TAPS), f32),
+            jax.ShapeDtypeStruct((3 * (per + 2), 128), f32),
+            jax.ShapeDtypeStruct((8, 128), f32),
         ),
         in_specs=[VM],
         out_specs=(VM, VM, VM),
         scratch_shapes=[
-            pltpu.VMEM((2, rows), f32),
-            pltpu.VMEM((SLAB, 2, rows), f32),
-            pltpu.VMEM((SLAB, 2, rows), f32),
-            pltpu.VMEM((2, TAPS), f32),
-            pltpu.VMEM((2, TAPS), f32),
-            pltpu.VMEM((2, TAPS), f32),
-            pltpu.VMEM((2, TAPS), f32),
-            pltpu.VMEM((2, TAPS), f32),
+            pltpu.VMEM((2 * per, 128), f32),
+            pltpu.VMEM((2 * per, 128), f32),
+            pltpu.VMEM((SLAB, 2 * per, 128), f32),
+            pltpu.VMEM((SLAB, 2 * per, 128), f32),
+            pltpu.VMEM((2 * per, 128), f32),
+            pltpu.VMEM((2, 128), f32),
+            pltpu.VMEM((2 * per, 128), f32),
+            pltpu.VMEM((2, 128), f32),
+            pltpu.VMEM((2, 2, 128), f32),
             pltpu.VMEM((slabs, 12, 128), f32),
-            dma((3,)),
+            dma((1,)),
             dma((SLAB,)), dma((SLAB,)),
             dma((cols,)), dma((1,)),
             dma((1,)), dma((1,)),
             dma((SLAB,)), dma((SLAB,)),
             dma((SLAB,)), dma((1,)),
             dma((SLAB,)), dma((1,)),
-            dma((2, slabs)), dma((2,)),
+            dma((3, slabs)), dma((3,)),
             dma((slabs,)), dma((slabs,)),
+            pltpu.SemaphoreType.REGULAR((5,)),
         ],
         compiler_params=pltpu.CompilerParams(
             collective_id=0, has_side_effects=True, vmem_limit_bytes=8 * 2**20
@@ -459,14 +468,15 @@
 
 
 def remainder_kernel(
-    count, sums_ref, ext_ref, tail_ref, over_ref, coup_ref, panel_ref, panel2_ref, basis_ref, cross_ref, flip_ref
+    count, sums_ref, ext_ref, tail_ref, over_ref, coup_ref, panel_ref, panel2_ref, basis_ref, cross_ref
 ):
-    blocks = (ext_ref.shape[1]) // 128
+    blocks = ext_ref.shape[0] // 3
     steps = blocks - 2
     parts = 128 * steps // 512
 
     def late(t):
-        tail = jnp.where(iota((1, TAPS), 1) == 0, 0.0, tail_ref[t : t + 1, :])
+        rows = tail_ref[0:2, :] if t == 0 else dot(tail_ref[...], anti_identity())[2 * t : 2 * t + 2]
+        tail = jnp.where(iota((1, TAPS), 1) == 0, 0.0, jnp.concatenate([rows[0:1], rows[1:2]], axis=1))
         row = jnp.concatenate([jnp.zeros((1, 128), jnp.float32), tail], axis=1)
         turned = pltpu.roll(jnp.broadcast_to(row, (128, 384)), 0, 1, stride=1, stride_axis=0)
         return turned[:, 128:256], turned[:, 256:384]
@@ -487,16 +497,10 @@
         got["gram21"] = thirds((gram_low[:, :128] + dot6(near6, far6)) / count)
         got["gram22"] = (gram_low[:, 128:] + near_near) / count
 
-    def turn_around():
-        ext = jnp.concatenate(
-            [ext_ref[t : t + 1, 128 * b : 128 * b + 128] for t in range(3) for b in range(blocks)], axis=0
-        )
-        flip_ref[0 : 3 * blocks, :] = dot(ext, anti_identity())
-
     def toeplitz(t):
         def piece():
             row = jnp.concatenate(
-                [flip_ref[blocks * t + b : blocks * t + b + 1, :] for b in reversed(range(blocks))], axis=1
+                [ext_ref[blocks * t + b : blocks * t + b + 1, :] for b in reversed(range(blocks))], axis=1
             )
             turned = pltpu.roll(jnp.broadcast_to(row, (128, 128 * blocks)), 1, 1, stride=1, stride_axis=0)
             for k in range(2):
@@ -527,7 +531,7 @@
     first = jnp.concatenate(
         factor_inverse(
             [gram11[8 * i : 8 * i + 8] for i in range(16)],
-            [gram_rest, turn_around] + [toeplitz(t) for t in range(3)] + [cross(1 + t) for t in range(2)],
+            [gram_rest] + [toeplitz(t) for t in range(3)] + [cross(1 + t) for t in range(2)],
         ),
         axis=0,
     )
@@ -600,7 +604,7 @@
 
 
 def remainder(sums, ext, tail, count):
-    rows = ext.shape[1] - TAPS
+    rows = 128 * (ext.shape[0] // 3) - TAPS
     f32 = jnp.float32
     return pl.pallas_call(
         functools.partial(remainder_kernel, count),
@@ -613,7 +617,6 @@
             pltpu.VMEM((rows, 128), f32),
             pltpu.VMEM((rows, 128), f32),
             pltpu.VMEM((WIDE, 512), f32),
-            pltpu.VMEM((24, 128), f32),
         ],
         compiler_params=pltpu.CompilerParams(vmem_limit_bytes=24 * 2**20),
     )(sums, ext, tail)

time: 43.4 us -> 40.3 us (0.929)
  Pallas kernels: 41.9 us -> 38.9 us
    pallas_call x1, Pallas kernels: 32.9 us -> 29.8 us  [lag_sums(): pl.pallas_call(functools.partial(lag_kernel, slabs, cols), name='lag_sums...]
where the time goes in v3:
time: 40.3 us; the launch traced here: 40.2 us
  Pallas kernels  38.9 us (97%)
  local copies, waits for them, and re-layouts  0.68 us (2%)
  between operations  0.65 us (2%)
    pallas_call x1, Pallas kernels, lag_sums(): pl.pallas_call(functools.partial(lag_kernel, slabs, cols), name='lag_sums...  29.8 us
    pallas_call x1, Pallas kernels, remainder(): pl.pallas_call(functools.partial(remainder_kernel, count), name='remainde...  9.04 us

profile of v3, /device:TPU:2, one launch (start us, length us, event | category | flops | bytes accessed | tf_op | source)
XLA Modules:
  0.0 40.2 jit_solution(15594899535601793831)
XLA Ops:
  0.6 0.0 copy-start
  0.6 0.7 %copy-done = f32[2,512]{1,0:T(2,128)S(1)} copy-done((f32[2,512]{1,0:T(2,128)S(1)}, f32[2,512]{1,0:T(2,128)}, u32[]{:S(2)}) %copy-start) | copy-done | bytes 4120
  1.3 29.8 %lag_sums.1 = (f32[12,128]{1,0:T(8,128)S(1)}, f32[18,128]{1,0:T(8,128)S(1)}, f32[8,128]{1,0:T(8,128)S(1)}) custom-call(f32[2,512]{1,0:T(2,128)S(1)} %copy-done), custom_call_target="tpu_custom_call" | custom-call | tf_op jit(solution)/shard_map/lag_sums/pallas_call | solution.py:315
  31.2 9.0 %remainder.1 = (f32[512,512]{1,0:T(8,128)}, f32[256,512]{1,0:T(8,128)}) custom-call(f32[12,128]{1,0:T(8,128)S(1)} %get-tuple-element.5.sums_ref, f32[18,128]{1,0:T(8,128)S(1)} %get-tuple-element.6.ext_ref, f32[8,128]{1,0:T(8,128)S(1)} %get-tuple-element.7.tail_ref), custom_call_target="tpu_custom_call" | custom-call | tf_op jit(solution)/shard_map/remainder/pallas_call | solution.py:609
Async XLA Ops:
  0.6 0.7 %copy-start = (f32[2,512]{1,0:T(2,128)S(1)}, f32[2,512]{1,0:T(2,128)}, u32[]{:S(2)}) copy-start(f32[2,512]{1,0:T(2,128)} %x_ref.1) | copy-start | bytes 12292

commit v4 on v3

--- a/solution.py
+++ b/solution.py
@@ -31,11 +31,13 @@
 
 def lag_kernel(
     slabs, cols,
-    x_ref, sums_ref, ext_ref, tail_ref,
-    mine, own0, slab0, slabc, before0, after0, beforec, late0, latec, lags,
+    x_hbm, sums_ref, late_ref, panel_ref, block_ref,
+    x_ref, ext_ref, mine, own0, slab0, slabc, before0, after0, beforec, late0, latec, lags,
     local_sem, send_x, recv_x, send_0, recv_0, send_hc, recv_hc,
     send_s0, recv_s0, send_hb, recv_hb, send_ha, recv_ha, send_t, recv_t, send_l, recv_l, hello,
 ):
+    fetch = pltpu.make_async_copy(x_hbm, x_ref, local_sem.at[1])
+    fetch.start()
     row, col = lax.axis_index("row"), lax.axis_index("col")
     z, y = row // SLAB, row % SLAB
     per = x_ref.shape[1] // 128
@@ -110,6 +112,7 @@
     def _():
         after0[...] = jnp.zeros_like(after0)
 
+    fetch.wait()
     plain = jnp.concatenate(
         [x_ref[t : t + 1, 128 * b : 128 * b + 128] for t in range(2) for b in range(per)], axis=0
     )
@@ -184,6 +187,30 @@
     @pl.when(has_after)
     def _():
         remote(own0.at[0:2], after0, send_ha.at[0], recv_ha.at[0], at(z, y, col)).wait_recv()
+
+    def all_came():
+        if reach:
+            pl.semaphore_wait(hello.at[len(reach) - 1], 2)
+
+    def tails(k):
+        return (
+            remote(slab0.at[SLAB - 1, per - 2 : per], late0, send_t.at[0, k], recv_t.at[0], around(k)),
+            remote(slabc.at[SLAB - 1, per - 2 : per], latec.at[0], send_t.at[1, k], recv_t.at[1], around(k)),
+            remote(slabc.at[SLAB - 1, 2 * per - 2 :], latec.at[1], send_t.at[2, k], recv_t.at[2], around(k)),
+        )
+
+    @pl.when(in_tail)
+    def _():
+        all_came()
+
+        @pl.loop(1, slabs)
+        def _(k):
+            for copy in tails(k):
+                copy.start()
+
+        late0[...] = slab0[SLAB - 1, per - 2 : per]
+        latec[0] = slabc[SLAB - 1, per - 2 : per]
+        latec[1] = slabc[SLAB - 1, 2 * per - 2 :]
 
     count = SLAB * per
     ext0 = jnp.concatenate([before0[per - 2 : per, :]] + [slab0[j, :per, :] for j in range(SLAB)] + [after0[...]], axis=0)
@@ -209,33 +236,14 @@
         for b in range(4):
             lags[z, 4 * t + b : 4 * t + b + 1, :] = summed[:, 128 + 128 * b : 256 + 128 * b]
 
-    if reach:
-        pl.semaphore_wait(hello.at[len(reach) - 1], 2)
-
     def exchange(k):
         return remote(lags.at[z], lags.at[z], send_l.at[k], recv_l.at[z], around(k))
+
+    pl.when(z < slabs - 1)(all_came)
 
     @pl.loop(0, slabs - 1)
     def _(k):
         exchange(1 + (k + slabs // 2 - 1) % (slabs - 1)).start()
-
-    def tails(k):
-        return (
-            remote(slab0.at[SLAB - 1, per - 2 : per], late0, send_t.at[0, k], recv_t.at[0], around(k)),
-            remote(slabc.at[SLAB - 1, per - 2 : per], latec.at[0], send_t.at[1, k], recv_t.at[1], around(k)),
-            remote(slabc.at[SLAB - 1, 2 * per - 2 :], latec.at[1], send_t.at[2, k], recv_t.at[2], around(k)),
-        )
-
-    @pl.when(in_tail)
-    def _():
-        @pl.loop(1, slabs)
-        def _(k):
-            for copy in tails(k):
-                copy.start()
-
-        late0[...] = slab0[SLAB - 1, per - 2 : per]
-        latec[0] = slabc[SLAB - 1, per - 2 : per]
-        latec[1] = slabc[SLAB - 1, 2 * per - 2 :]
 
     reach_back = per + 2
     ext_ref[2:reach_back, :] = own0[per:, :]
@@ -259,15 +267,48 @@
         for t in range(2):
             ext_ref[reach_back * (t + 1) : reach_back * (t + 1) + 2, :] = slabc[before, per * t + per - 2 : per * t + per, :]
 
+    for t in range(3):
+        line = jnp.concatenate(
+            [ext_ref[reach_back * t + b : reach_back * t + b + 1, :] for b in reversed(range(reach_back))], axis=1
+        )
+        spun = pltpu.roll(jnp.broadcast_to(line, (128, 128 * reach_back)), 1, 1, stride=1, stride_axis=0)
+        for k in range(2):
+            for s in range(per):
+                block = spun[:, 512 + 128 * (k - s) : 640 + 128 * (k - s)]
+                if t == 0:
+                    panel_ref[128 * s : 128 * s + 128, 128 * k : 128 * k + 128] = block
+                else:
+                    block_ref[128 * s : 128 * s + 128, 256 * (t - 1) + 128 * k : 256 * (t - 1) + 128 * k + 128] = block
+
     @pl.when(z < slabs - 1)
     def _():
         for copy in tails(0):
             copy.wait_recv()
 
-    tail_ref[0:2, :] = late0[...]
-    tail_ref[2:4, :] = latec[0]
-    tail_ref[4:6, :] = latec[1]
-    tail_ref[6:8, :] = jnp.zeros((2, 128), jnp.float32)
+    ends = jnp.concatenate([latec[0], latec[1], jnp.zeros((4, 128), jnp.float32)], axis=0)
+    forward = dot(ends, anti_identity())
+
+    def late_rows(t):
+        rows = late0[...] if t == 0 else forward[2 * t - 2 : 2 * t]
+        tail = jnp.where(iota((1, TAPS), 1) == 0, 0.0, jnp.concatenate([rows[0:1], rows[1:2]], axis=1))
+        line = jnp.concatenate([jnp.zeros((1, 128), jnp.float32), tail], axis=1)
+        spun = pltpu.roll(jnp.broadcast_to(line, (128, 384)), 0, 1, stride=1, stride_axis=0)
+        return spun[:, 128:256], spun[:, 256:384]
+
+    near0, far0 = late_rows(0)
+    near6, far6 = thirds(near0), thirds(far0)
+    near_near = dot6(near6, near6)
+    late_ref[:128, :128] = near_near + dot6(far6, far6)
+    late_ref[128:, :128] = dot6(near6, far6)
+    late_ref[128:, 128:256] = near_near
+    near_a, far_a = split(near0), split(far0)
+    for t in (1, 2):
+        near_c, far_c = (split(v) for v in late_rows(t))
+        same = dot3(near_a, near_c, True)
+        late_ref[:128, 256 * t : 256 * t + 128] = same + dot3(far_a, far_c, True)
+        late_ref[:128, 256 * t + 128 : 256 * t + 256] = dot3(far_a, near_c, True)
+        late_ref[128:, 256 * t : 256 * t + 128] = dot3(near_a, far_c, True)
+        late_ref[128:, 256 * t + 128 : 256 * t + 256] = same
 
     @pl.loop(1, slabs)
     def _(k):
@@ -310,19 +351,23 @@
 
 
 def lag_sums(traces, slabs, cols):
-    per = traces.shape[1] // 128
+    rows = traces.shape[1]
+    per = rows // 128
     f32, dma = jnp.float32, pltpu.SemaphoreType.DMA
     return pl.pallas_call(
         functools.partial(lag_kernel, slabs, cols),
         name="lag_sums",
         out_shape=(
             jax.ShapeDtypeStruct((12, 128), f32),
-            jax.ShapeDtypeStruct((3 * (per + 2), 128), f32),
-            jax.ShapeDtypeStruct((8, 128), f32),
+            jax.ShapeDtypeStruct((WIDE, WIDE + 2 * TAPS), f32),
+            jax.ShapeDtypeStruct((rows, WIDE), f32),
+            jax.ShapeDtypeStruct((rows, 2 * TAPS), f32),
         ),
-        in_specs=[VM],
-        out_specs=(VM, VM, VM),
+        in_specs=[pl.BlockSpec(memory_space=pltpu.HBM)],
+        out_specs=(VM, VM, VM, VM),
         scratch_shapes=[
+            pltpu.VMEM((2, rows), f32),
+            pltpu.VMEM((3 * (per + 2), 128), f32),
             pltpu.VMEM((2 * per, 128), f32),
             pltpu.VMEM((2 * per, 128), f32),
             pltpu.VMEM((SLAB, 2 * per, 128), f32),
@@ -333,7 +378,7 @@
             pltpu.VMEM((2, 128), f32),
             pltpu.VMEM((2, 2, 128), f32),
             pltpu.VMEM((slabs, 12, 128), f32),
-            dma((1,)),
+            dma((2,)),
             dma((SLAB,)), dma((SLAB,)),
             dma((cols,)), dma((1,)),
             dma((1,)), dma((1,)),
@@ -345,7 +390,7 @@
             pltpu.SemaphoreType.REGULAR((5,)),
         ],
         compiler_params=pltpu.CompilerParams(
-            collective_id=0, has_side_effects=True, vmem_limit_bytes=8 * 2**20
+            collective_id=0, has_side_effects=True, vmem_limit_bytes=12 * 2**20
         ),
     )(traces)
 
@@ -468,70 +513,37 @@
 
 
 def remainder_kernel(
-    count, sums_ref, ext_ref, tail_ref, over_ref, coup_ref, panel_ref, panel2_ref, basis_ref, cross_ref
+    count, sums_ref, late_ref, panel_ref, block_ref, over_hbm, coup_hbm,
+    over_ref, coup_ref, panel2_ref, basis_ref, cross_ref, sem,
 ):
-    blocks = ext_ref.shape[0] // 3
-    steps = blocks - 2
+    steps = panel_ref.shape[0] // 128
     parts = 128 * steps // 512
-
-    def late(t):
-        rows = tail_ref[0:2, :] if t == 0 else dot(tail_ref[...], anti_identity())[2 * t : 2 * t + 2]
-        tail = jnp.where(iota((1, TAPS), 1) == 0, 0.0, jnp.concatenate([rows[0:1], rows[1:2]], axis=1))
-        row = jnp.concatenate([jnp.zeros((1, 128), jnp.float32), tail], axis=1)
-        turned = pltpu.roll(jnp.broadcast_to(row, (128, 384)), 0, 1, stride=1, stride_axis=0)
-        return turned[:, 128:256], turned[:, 256:384]
 
     def early(t):
         row = jnp.concatenate([sums_ref[4 * t + b : 4 * t + b + 1, :] for b in range(4)], axis=1)
         turned = pltpu.roll(jnp.broadcast_to(row, (128, 512)), 0, 1, stride=1, stride_axis=0)
         return turned[:, 256:512], turned[:, 128:384]
 
-    near0, far0 = late(0)
     gram_top, gram_low = early(0)
-    near6, far6 = thirds(near0), thirds(far0)
-    near_near = dot6(near6, near6)
-    gram11 = (gram_top[:, :128] + (near_near + dot6(far6, far6))) / count
+    gram11 = (gram_top[:, :128] + late_ref[:128, :128]) / count
     got = {}
 
     def gram_rest():
-        got["gram21"] = thirds((gram_low[:, :128] + dot6(near6, far6)) / count)
-        got["gram22"] = (gram_low[:, 128:] + near_near) / count
-
-    def toeplitz(t):
-        def piece():
-            row = jnp.concatenate(
-                [ext_ref[blocks * t + b : blocks * t + b + 1, :] for b in reversed(range(blocks))], axis=1
-            )
-            turned = pltpu.roll(jnp.broadcast_to(row, (128, 128 * blocks)), 1, 1, stride=1, stride_axis=0)
-            for k in range(2):
-                for s in range(steps):
-                    rows, at = slice(128 * s, 128 * s + 128), 128 * k
-                    block = turned[:, 512 + 128 * (k - s) : 640 + 128 * (k - s)]
-                    if t == 0:
-                        panel_ref[rows, at : at + 128] = block
-                    else:
-                        over_ref[rows, 256 * (t - 1) + at : 256 * (t - 1) + at + 128] = block
-
-        return piece
+        got["gram21"] = thirds((gram_low[:, :128] + late_ref[128:, :128]) / count)
+        got["gram22"] = (gram_low[:, 128:] + late_ref[128:, 128:256]) / count
 
     def cross(t):
         def piece():
-            near, far = late(t)
             top, low = early(t)
-            near_a, far_a, near_c, far_c = split(near0), split(far0), split(near), split(far)
-            same = dot3(near_a, near_c, True)
-            at = 256 * (t - 1)
-            cross_ref[:128, at : at + 128] = (top[:, :128] + (same + dot3(far_a, far_c, True))) / count
-            cross_ref[:128, at + 128 : at + 256] = (top[:, 128:] + dot3(far_a, near_c, True)) / count
-            cross_ref[128:, at : at + 128] = (low[:, :128] + dot3(near_a, far_c, True)) / count
-            cross_ref[128:, at + 128 : at + 256] = (low[:, 128:] + same) / count
+            cross_ref[:128, 256 * (t - 1) : 256 * t] = (top + late_ref[:128, 256 * t : 256 * t + 256]) / count
+            cross_ref[128:, 256 * (t - 1) : 256 * t] = (low + late_ref[128:, 256 * t : 256 * t + 256]) / count
 
         return piece
 
     first = jnp.concatenate(
         factor_inverse(
             [gram11[8 * i : 8 * i + 8] for i in range(16)],
-            [gram_rest] + [toeplitz(t) for t in range(3)] + [cross(1 + t) for t in range(2)],
+            [gram_rest] + [cross(1 + t) for t in range(2)],
         ),
         axis=0,
     )
@@ -573,7 +585,7 @@
     def project(s, i):
         def piece():
             change = dot3(split(basis_ref[upper(s), :]), split(coup_ref[:128, wide(i)]))
-            over_ref[upper(s), wide(i)] = over_ref[upper(s), wide(i)] - change
+            over_ref[upper(s), wide(i)] = block_ref[upper(s), wide(i)] - change
 
         return piece
 
@@ -590,36 +602,47 @@
     )
     second2 = split(second)
     basis2 = dot3(split(panel2_ref[...]), second2, True)
-    panel2_ref[...] = basis2
     basis2s = split(basis2)
-    for i in range(2):
+    out = []
+    for i in (1, 0):
         coup2 = dot3(second2, split(cross_ref[128:, wide(i)]))
         coup_ref[128:, wide(i)] = coup2
+        if i == 0:
+            out.append(pltpu.make_async_copy(coup_ref, coup_hbm, sem.at[2]))
+            out[-1].start()
         over_ref[:, wide(i)] = over_ref[:, wide(i)] - dot3(basis2s, split(coup2))
-
-    @pl.when(lax.axis_index("col") == 0)
-    def _():
-        over_ref[:, :128] = basis_ref[...]
-        over_ref[:, 128:WIDE] = panel2_ref[...]
-
-
-def remainder(sums, ext, tail, count):
-    rows = 128 * (ext.shape[0] // 3) - TAPS
-    f32 = jnp.float32
+        if i == 0:
+
+            @pl.when(lax.axis_index("col") == 0)
+            def _():
+                over_ref[:, :128] = basis_ref[...]
+                over_ref[:, 128:WIDE] = basis2
+
+        out.append(pltpu.make_async_copy(over_ref.at[:, wide(i)], over_hbm.at[:, wide(i)], sem.at[i]))
+        out[-1].start()
+    for copy in out:
+        copy.wait()
+
+
+def remainder(sums, late, panel, block, count):
+    rows, f32 = panel.shape[0], jnp.float32
+    anywhere = pl.BlockSpec(memory_space=pl.ANY)
     return pl.pallas_call(
         functools.partial(remainder_kernel, count),
         name="remainder",
         out_shape=(jax.ShapeDtypeStruct((rows, 512), f32), jax.ShapeDtypeStruct((WIDE, 512), f32)),
-        in_specs=[VM, VM, VM],
-        out_specs=(VM, VM),
+        in_specs=[VM, VM, VM, VM],
+        out_specs=(anywhere, anywhere),
         scratch_shapes=[
-            pltpu.VMEM((rows, WIDE), f32),
+            pltpu.VMEM((rows, 512), f32),
+            pltpu.VMEM((WIDE, 512), f32),
             pltpu.VMEM((rows, 128), f32),
             pltpu.VMEM((rows, 128), f32),
             pltpu.VMEM((WIDE, 512), f32),
+            pltpu.SemaphoreType.DMA((3,)),
         ],
         compiler_params=pltpu.CompilerParams(vmem_limit_bytes=24 * 2**20),
-    )(sums, ext, tail)
+    )(sums, late, panel, block)
 
 
 def solution(mesh):
@@ -627,8 +650,8 @@
 
     def body(traces):
         count = traces.shape[1] * slabs * SLAB
-        sums, ext, tail = lag_sums(traces, slabs, cols)
-        return remainder(sums, ext, tail, count)
+        held = pltpu.with_memory_space_constraint(traces, pltpu.HBM)
+        return remainder(*lag_sums(held, slabs, cols), count)
 
     return jax.shard_map(
         body,

time: 40.3 us -> 39.5 us (0.980)
  local copies, waits for them, and re-layouts: 0.68 us -> 0 us
    unnamed x2 -> x0, local copies, waits for them, and re-layouts: 0.68 us -> none
where the time goes in v4:
time: 39.5 us; the launch traced here: 39.3 us
  Pallas kernels  38.7 us (98%)
  between operations  0.64 us (2%)
    pallas_call x1, Pallas kernels, lag_sums(): pl.pallas_call(functools.partial(lag_kernel, slabs, cols), name='lag_sums...  29.8 us
    pallas_call x1, Pallas kernels, remainder(): pl.pallas_call(functools.partial(remainder_kernel, count), name='remainde...  8.84 us

profile of v4, /device:TPU:2, one launch (start us, length us, event | category | flops | bytes accessed | tf_op | source)
XLA Modules:
  0.0 39.3 jit_solution(15576769885951786526)
XLA Ops:
  0.6 29.8 %lag_sums.1 = (f32[12,128]{1,0:T(8,128)S(1)}, f32[256,768]{1,0:T(8,128)S(1)}, f32[512,256]{1,0:T(8,128)S(1)}, f32[512,512]{1,0:T(8,128)S(1)}) custom-call(f32[2,512]{1,0:T(2,128)} %x_hbm.1), custom_call_target="tpu_custom_call" | custom-call | tf_op jit(solution)/shard_map/lag_sums/pallas_call | solution.py:357
  30.5 8.8 %remainder.1 = (f32[512,512]{1,0:T(8,128)}, f32[256,512]{1,0:T(8,128)}) custom-call(f32[12,128]{1,0:T(8,128)S(1)} %get-tuple-element.6.sums_ref, f32[256,768]{1,0:T(8,128)S(1)} %get-tuple-element.7.late_ref, f32[512,256]{1,0:T(8,128)S(1)} %get-tuple-element.8.panel_ref, f32[512,512]{1,0:T(8,128)S(1)} %get-tuple-element.9.block_ref), custom_call_target="tpu_custom_call" | custom-call | tf_op jit(solution)/shard_map/remainder/pallas_call | solution.py:630

commit v5 on v4

--- a/solution.py
+++ b/solution.py
@@ -231,13 +231,14 @@
         )
     table = outer6(thirds(jnp.concatenate(lefts, axis=1)), thirds(right))
     for t in range(3):
-        skewed = pltpu.roll(table[128 * t : 128 * t + 128], 1, 1, stride=1, stride_axis=0)
+        skewed = pltpu.roll(table[128 * t : 128 * t + 128], min(t, 1), 1, stride=1, stride_axis=0)
         summed = jnp.sum(skewed, axis=0, keepdims=True)
-        for b in range(4):
-            lags[z, 4 * t + b : 4 * t + b + 1, :] = summed[:, 128 + 128 * b : 256 + 128 * b]
+        at_row = max(4 * t - 2, 0)
+        for b in range(2 if t == 0 else 4):
+            lags[z, at_row + b : at_row + b + 1, :] = summed[:, 128 + 128 * b : 256 + 128 * b]
 
     def exchange(k):
-        return remote(lags.at[z], lags.at[z], send_l.at[k], recv_l.at[z], around(k))
+        return remote(lags.at[z], lags.at[z], send_l.at[k], recv_l.at[0], around(k))
 
     pl.when(z < slabs - 1)(all_came)
 
@@ -310,13 +311,6 @@
         late_ref[128:, 256 * t : 256 * t + 128] = dot3(near_a, far_c, True)
         late_ref[128:, 256 * t + 128 : 256 * t + 256] = same
 
-    @pl.loop(1, slabs)
-    def _(k):
-        other = (z + k) % slabs
-        remote(lags.at[other], lags.at[other], send_l.at[k], recv_l.at[other], at(other, y, col)).wait_recv()
-
-    sums_ref[...] = tree([lags[k] for k in range(slabs)])
-
     @pl.when(col == 0)
     def _():
         for k in range(1, cols):
@@ -348,6 +342,11 @@
     @pl.loop(1, slabs)
     def _(k):
         exchange(k).wait_send()
+
+    others = lags.at[pl.ds(0, slabs - 1)]
+    remote(others, others, send_l.at[0], recv_l.at[0], around(1)).wait_recv()
+
+    sums_ref[...] = tree([lags[k] for k in range(slabs)])
 
 
 def lag_sums(traces, slabs, cols):
@@ -358,7 +357,7 @@
         functools.partial(lag_kernel, slabs, cols),
         name="lag_sums",
         out_shape=(
-            jax.ShapeDtypeStruct((12, 128), f32),
+            jax.ShapeDtypeStruct((10, 128), f32),
             jax.ShapeDtypeStruct((WIDE, WIDE + 2 * TAPS), f32),
             jax.ShapeDtypeStruct((rows, WIDE), f32),
             jax.ShapeDtypeStruct((rows, 2 * TAPS), f32),
@@ -377,7 +376,7 @@
             pltpu.VMEM((2 * per, 128), f32),
             pltpu.VMEM((2, 128), f32),
             pltpu.VMEM((2, 2, 128), f32),
-            pltpu.VMEM((slabs, 12, 128), f32),
+            pltpu.VMEM((slabs, 10, 128), f32),
             dma((2,)),
             dma((SLAB,)), dma((SLAB,)),
             dma((cols,)), dma((1,)),
@@ -520,17 +519,22 @@
     parts = 128 * steps // 512
 
     def early(t):
-        row = jnp.concatenate([sums_ref[4 * t + b : 4 * t + b + 1, :] for b in range(4)], axis=1)
+        row = jnp.concatenate([sums_ref[4 * t - 2 + b : 4 * t - 1 + b, :] for b in range(4)], axis=1)
         turned = pltpu.roll(jnp.broadcast_to(row, (128, 512)), 0, 1, stride=1, stride_axis=0)
         return turned[:, 256:512], turned[:, 128:384]
 
-    gram_top, gram_low = early(0)
-    gram11 = (gram_top[:, :128] + late_ref[:128, :128]) / count
+    half = jnp.concatenate([sums_ref[0:1, :], sums_ref[1:2, :], jnp.zeros((1, 128), jnp.float32)], axis=1)
+    spun = pltpu.roll(jnp.broadcast_to(half, (128, 384)), 1, 1, stride=1, stride_axis=0)
+    below_diagonal = spun[:, 256:384]
+    gram_near = jnp.where(
+        iota((128, 128), 0) >= iota((128, 128), 1), below_diagonal, jnp.transpose(below_diagonal)
+    )
+    gram11 = (gram_near + late_ref[:128, :128]) / count
     got = {}
 
     def gram_rest():
-        got["gram21"] = thirds((gram_low[:, :128] + late_ref[128:, :128]) / count)
-        got["gram22"] = (gram_low[:, 128:] + late_ref[128:, 128:256]) / count
+        got["gram21"] = thirds((spun[:, 128:256] + late_ref[128:, :128]) / count)
+        got["gram22"] = (gram_near + late_ref[128:, 128:256]) / count
 
     def cross(t):
         def piece():

time: 39.5 us -> 39.1 us (0.990)
  Pallas kernels: 38.7 us -> 38.2 us
    pallas_call x1, Pallas kernels: 29.8 us -> 29.3 us  [lag_sums(): pl.pallas_call(functools.partial(lag_kernel, slabs, cols), name='lag_sums...]
where the time goes in v5:
time: 39.1 us; the launch traced here: 38.9 us
  Pallas kernels  38.2 us (98%)
  between operations  0.64 us (2%)
    pallas_call x1, Pallas kernels, lag_sums(): pl.pallas_call(functools.partial(lag_kernel, slabs, cols), name='lag_sums...  29.3 us
    pallas_call x1, Pallas kernels, remainder(): pl.pallas_call(functools.partial(remainder_kernel, count), name='remainde...  8.97 us

profile of v5, /device:TPU:2, one launch (start us, length us, event | category | flops | bytes accessed | tf_op | source)
XLA Modules:
  0.0 38.9 jit_solution(11829307332535664799)
XLA Ops:
  0.6 29.3 %lag_sums.1 = (f32[10,128]{1,0:T(8,128)S(1)}, f32[256,768]{1,0:T(8,128)S(1)}, f32[512,256]{1,0:T(8,128)S(1)}, f32[512,512]{1,0:T(8,128)S(1)}) custom-call(f32[2,512]{1,0:T(2,128)} %x_hbm.1), custom_call_target="tpu_custom_call" | custom-call | tf_op jit(solution)/shard_map/lag_sums/pallas_call | solution.py:356
  29.9 9.0 %remainder.1 = (f32[512,512]{1,0:T(8,128)}, f32[256,512]{1,0:T(8,128)}) custom-call(f32[10,128]{1,0:T(8,128)S(1)} %get-tuple-element.6.sums_ref, f32[256,768]{1,0:T(8,128)S(1)} %get-tuple-element.7.late_ref, f32[512,256]{1,0:T(8,128)S(1)} %get-tuple-element.8.panel_ref, f32[512,512]{1,0:T(8,128)S(1)} %get-tuple-element.9.block_ref), custom_call_target="tpu_custom_call" | custom-call | tf_op jit(solution)/shard_map/remainder/pallas_call | solution.py:634

commit v6 on v5

--- a/solution.py
+++ b/solution.py
@@ -612,18 +612,25 @@
         coup2 = dot3(second2, split(cross_ref[128:, wide(i)]))
         coup_ref[128:, wide(i)] = coup2
         if i == 0:
-            out.append(pltpu.make_async_copy(coup_ref, coup_hbm, sem.at[2]))
+            out.append(pltpu.make_async_copy(coup_ref, coup_hbm, sem.at[3]))
             out[-1].start()
-        over_ref[:, wide(i)] = over_ref[:, wide(i)] - dot3(basis2s, split(coup2))
-        if i == 0:
-
-            @pl.when(lax.axis_index("col") == 0)
-            def _():
-                over_ref[:, :128] = basis_ref[...]
-                over_ref[:, 128:WIDE] = basis2
-
-        out.append(pltpu.make_async_copy(over_ref.at[:, wide(i)], over_hbm.at[:, wide(i)], sem.at[i]))
-        out[-1].start()
+        coup2s = split(coup2)
+        height = over_ref.shape[0] // (2 - i)
+        for part in range(2 - i):
+            rows = slice(height * part, height * part + height)
+            change = dot3([v[rows] for v in basis2s], coup2s)
+            over_ref[rows, wide(i)] = over_ref[rows, wide(i)] - change
+            if i == 0:
+
+                @pl.when(lax.axis_index("col") == 0)
+                def _():
+                    over_ref[rows, :128] = basis_ref[rows, :]
+                    over_ref[rows, 128:WIDE] = basis2[rows]
+
+            out.append(
+                pltpu.make_async_copy(over_ref.at[rows, wide(i)], over_hbm.at[rows, wide(i)], sem.at[2 * i + part])
+            )
+            out[-1].start()
     for copy in out:
         copy.wait()
 
@@ -643,7 +650,7 @@
             pltpu.VMEM((rows, 128), f32),
             pltpu.VMEM((rows, 128), f32),
             pltpu.VMEM((WIDE, 512), f32),
-            pltpu.SemaphoreType.DMA((3,)),
+            pltpu.SemaphoreType.DMA((4,)),
         ],
         compiler_params=pltpu.CompilerParams(vmem_limit_bytes=24 * 2**20),
     )(sums, late, panel, block)

time: 39.1 us -> 39.2 us (level)
  the two profiles are of different devices: /device:TPU:2 before, /device:TPU:4 now
where the time goes in v6:
time: 39.2 us; the launch traced here: 39 us
  Pallas kernels  38.4 us (98%)
  between operations  0.64 us (2%)
    pallas_call x1, Pallas kernels, lag_sums(): pl.pallas_call(functools.partial(lag_kernel, slabs, cols), name='lag_sums...  29.4 us
    pallas_call x1, Pallas kernels, remainder(): pl.pallas_call(functools.partial(remainder_kernel, count), name='remainde...  8.98 us

profile of v6, /device:TPU:4, one launch (start us, length us, event | category | flops | bytes accessed | tf_op | source)
XLA Modules:
  0.0 39.0 jit_solution(2432069653184186518)
XLA Ops:
  0.6 29.4 %lag_sums.1 = (f32[10,128]{1,0:T(8,128)S(1)}, f32[256,768]{1,0:T(8,128)S(1)}, f32[512,256]{1,0:T(8,128)S(1)}, f32[512,512]{1,0:T(8,128)S(1)}) custom-call(f32[2,512]{1,0:T(2,128)} %x_hbm.1), custom_call_target="tpu_custom_call" | custom-call | tf_op jit(solution)/shard_map/lag_sums/pallas_call | solution.py:356
  30.0 9.0 %remainder.1 = (f32[512,512]{1,0:T(8,128)}, f32[256,512]{1,0:T(8,128)}) custom-call(f32[10,128]{1,0:T(8,128)S(1)} %get-tuple-element.6.sums_ref, f32[256,768]{1,0:T(8,128)S(1)} %get-tuple-element.7.late_ref, f32[512,256]{1,0:T(8,128)S(1)} %get-tuple-element.8.panel_ref, f32[512,512]{1,0:T(8,128)S(1)} %get-tuple-element.9.block_ref), custom_call_target="tpu_custom_call" | custom-call | tf_op jit(solution)/shard_map/remainder/pallas_call | solution.py:641

commit v7 on v5

--- a/solution.py
+++ b/solution.py
@@ -242,9 +242,8 @@
 
     pl.when(z < slabs - 1)(all_came)
 
-    @pl.loop(0, slabs - 1)
-    def _(k):
-        exchange(1 + (k + slabs // 2 - 1) % (slabs - 1)).start()
+    for k in sorted(range(1, slabs), key=lambda k: -min(k, slabs - k)):
+        exchange(k).start()
 
     reach_back = per + 2
     ext_ref[2:reach_back, :] = own0[per:, :]

time: 39.1 us -> 37.7 us (0.964)
  Pallas kernels: 38.2 us -> 36.9 us
    pallas_call x1, Pallas kernels: 29.3 us -> 27.9 us  [lag_sums(): pl.pallas_call(functools.partial(lag_kernel, slabs, cols), name='lag_sums...]
where the time goes in v7:
time: 37.7 us; the launch traced here: 37.5 us
  Pallas kernels  36.9 us (98%)
  between operations  0.64 us (2%)
    pallas_call x1, Pallas kernels, lag_sums(): pl.pallas_call(functools.partial(lag_kernel, slabs, cols), name='lag_sums...  27.9 us
    pallas_call x1, Pallas kernels, remainder(): pl.pallas_call(functools.partial(remainder_kernel, count), name='remainde...  8.97 us

profile of v7, /device:TPU:2, one launch (start us, length us, event | category | flops | bytes accessed | tf_op | source)
XLA Modules:
  0.0 37.5 jit_solution(15248571119909954187)
XLA Ops:
  0.6 27.9 %lag_sums.1 = (f32[10,128]{1,0:T(8,128)S(1)}, f32[256,768]{1,0:T(8,128)S(1)}, f32[512,256]{1,0:T(8,128)S(1)}, f32[512,512]{1,0:T(8,128)S(1)}) custom-call(f32[2,512]{1,0:T(2,128)} %x_hbm.1), custom_call_target="tpu_custom_call" | custom-call | tf_op jit(solution)/shard_map/lag_sums/pallas_call | solution.py:355
  28.5 9.0 %remainder.1 = (f32[512,512]{1,0:T(8,128)}, f32[256,512]{1,0:T(8,128)}) custom-call(f32[10,128]{1,0:T(8,128)S(1)} %get-tuple-element.6.sums_ref, f32[256,768]{1,0:T(8,128)S(1)} %get-tuple-element.7.late_ref, f32[512,256]{1,0:T(8,128)S(1)} %get-tuple-element.8.panel_ref, f32[512,512]{1,0:T(8,128)S(1)} %get-tuple-element.9.block_ref), custom_call_target="tpu_custom_call" | custom-call | tf_op jit(solution)/shard_map/remainder/pallas_call | solution.py:633
